TPU v7x, 256 devices: a whole 4x4x8 slice. The times are simulated.
256 devices in a mesh: gx: 8 (over z), gy: 32 (over x, y, core).
Axes of the slice: x: 4, y: 4, z: 8, core: 2. Of those that a mesh axis runs over, the one named last changes fastest.
Arguments:
- sources: float32 [8192, 4, 256], P(('gx', 'gy')), may hold values from -1 to 1, as said below
- live_counts: int32 [8192], P(('gx', 'gy')), may hold values from 1 to 256, as said below
- densities: float32 [296, 8192], P(None, ('gx', 'gy')), may hold values from -0.75 to 0.75
- near_list: int32 [8192, 4], P(('gx', 'gy')), may hold values from 0 to 8191, as said below
- far_list: int32 [8192, 16], P(('gx', 'gy')), may hold values from 0 to 8191, as said below
- far_class: int32 [8192, 16], P(('gx', 'gy')), may hold values from 0 to 15
- coarse_list: int32 [8192, 8], P(('gx', 'gy')), may hold values from 0 to 1023
- coarse_class: int32 [8192, 8], P(('gx', 'gy')), may hold values from 0 to 15
- translations: float32 [16, 296, 296], replicated, may hold values from -0.375 to 0.375
- check_to_equiv: float32 [296, 296], replicated, may hold values from -0.375 to 0.375
- up_check_to_equiv: float32 [296, 296], replicated, may hold values from -0.375 to 0.375
- partial_check: float32 [256, 296, 64], P(('gx', 'gy')), may hold values from -0.1875 to 0.1875
- contrib_ids: int32 [256, 64], P(('gx', 'gy')), may hold values from 0 to 1023, as said below
Outputs:
- potential: float32 [8192, 256], P(('gx', 'gy'))
Inputs may be any that keep to these rules, and one draw needn't show every extreme that they name: `near_list`: entry 0 of a leaf's row is the leaf itself; the others are distinct other leaves whose numbers differ from it by at most 32. `far_list`: A leaf's entries are distinct other leaves whose numbers differ from it by at most 32. `live_counts`: some leaf holds exactly 256 live points. `sources`: rows 0 to 2 lie in -1 to 1. `contrib_ids`: row d names only shared octants s with d - 1 <= floor(s * 256 / 1024) <= d + 1; a number may repeat.
All inputs are finite; a program needn't handle non-finite values.
Results may differ from a plain program's by a relative error of at most 0.0003.
Values sent between devices are 32-bit elements; how exact they have to be, the bound alone decides.
A program may use at most 64 MiB of HBM per device.

v0:
```python
import math

import jax
import jax.numpy as jnp
import numpy as np
from jax import lax
from jax.sharding import PartitionSpec as P

ORDER = 8
SHARED = 1024


soft_sq = 0.0625
surface_half = 2.5
grid_side = 32


def extended(block, sides, width):
    for axis, dim in sides:
        count = lax.axis_size(axis)
        forward = [(i, i + 1) for i in range(count - 1)]
        backward = [(target, source) for source, target in forward]
        low = lax.ppermute(
            lax.slice_in_dim(block, block.shape[dim] - width, None, axis=dim), axis, forward
        )
        high = lax.ppermute(lax.slice_in_dim(block, 0, width, axis=dim), axis, backward)
        block = jnp.concatenate([low, block, high], axis=dim)
    return block


def surface_points(surf_order):
    ladder = np.arange(surf_order)
    first, second, third = np.meshgrid(ladder, ladder, ladder, indexing="ij")
    last_index = surf_order - 1
    on_edge = (
        (first == 0)
        | (first == last_index)
        | (second == 0)
        | (second == last_index)
        | (third == 0)
        | (third == last_index)
    )
    coords = np.stack([first[on_edge], second[on_edge], third[on_edge]]).astype(np.float32)
    return jnp.asarray(-surface_half + 2.0 * surface_half * coords / last_index, jnp.float32)


def leaf_centres(leaf_ids):
    across = leaf_ids % grid_side
    along = leaf_ids // grid_side % grid_side
    upward = leaf_ids // (grid_side * grid_side)
    return 2.0 * jnp.stack([across, along, upward], axis=1).astype(jnp.float32)


def near_block(targets, neighbours):
    gap_first = targets[:, None, 0, :, None] - neighbours[:, :, 0, None, :]
    gap_second = targets[:, None, 1, :, None] - neighbours[:, :, 1, None, :]
    gap_third = targets[:, None, 2, :, None] - neighbours[:, :, 2, None, :]
    kernel = lax.rsqrt(
        gap_first * gap_first + gap_second * gap_second + gap_third * gap_third + soft_sq
    )
    return jnp.sum(kernel * neighbours[:, :, 3, None, :], axis=(1, 3))


def far_block(local_pos, equiv_rows, surface):
    gap_first = local_pos[:, 0, :, None] - surface[0][None, None, :]
    gap_second = local_pos[:, 1, :, None] - surface[1][None, None, :]
    gap_third = local_pos[:, 2, :, None] - surface[2][None, None, :]
    kernel = lax.rsqrt(
        gap_first * gap_first + gap_second * gap_second + gap_third * gap_third + soft_sq
    )
    return jnp.sum(kernel * equiv_rows[:, None, :], axis=2)


def on_device(
    sources,
    live_counts,
    densities,
    near_list,
    far_list,
    far_class,
    coarse_list,
    coarse_class,
    translations,
    check_to_equiv,
    up_check_to_equiv,
    partial_check,
    contrib_ids,
):
    highest = lax.Precision.HIGHEST
    own_leaves = sources.shape[0]
    leaf_pts = sources.shape[2]
    device = lax.axis_index(("gx", "gy"))
    first_leaf = device * own_leaves
    window_start = first_leaf - own_leaves
    leaf_ids = first_leaf + jnp.arange(own_leaves, dtype=jnp.int32)
    centres = leaf_centres(leaf_ids)
    is_live = jnp.arange(leaf_pts, dtype=jnp.int32)[None, :] < live_counts[:, None]
    positions = sources[:, :3, :] + centres[:, :, None]
    charges = jnp.where(is_live, sources[:, 3, :], 0.0)
    packed = jnp.concatenate([positions, charges[:, None, :]], axis=1)
    window = extended(packed, ((("gx", "gy"), 0),), own_leaves)
    dens_window = extended(densities, ((("gx", "gy"), 1),), own_leaves)
    partial_value = partial_check[0]
    slot_ids = contrib_ids[0]
    octant_ids = jnp.arange(SHARED, dtype=jnp.int32)
    spread_hot = (slot_ids[:, None] == octant_ids[None, :]).astype(jnp.float32)
    local_dense = jnp.dot(
        partial_value, spread_hot, precision=highest, preferred_element_type=jnp.float32
    )
    up_check = lax.psum(local_dense, ("gx", "gy"))
    up_equiv = jnp.dot(
        up_check_to_equiv, up_check, precision=highest, preferred_element_type=jnp.float32
    )
    near_local = near_list - window_start
    step_leaves = math.gcd(own_leaves, 8)
    blocks = own_leaves // step_leaves

    def near_step(inputs):
        targets, chosen = inputs
        return near_block(targets, window[chosen])

    near_pot = lax.map(
        near_step,
        (
            positions.reshape(blocks, step_leaves, 3, leaf_pts),
            near_local.reshape(blocks, step_leaves, -1),
        ),
    )
    near_pot = near_pot.reshape(own_leaves, leaf_pts)
    class_ids = jnp.arange(translations.shape[0], dtype=jnp.int32)
    far_hot = (far_class[:, :, None] == class_ids[None, None, :]).astype(jnp.float32)
    coarse_hot = (coarse_class[:, :, None] == class_ids[None, None, :]).astype(jnp.float32)
    far_cols = dens_window[:, far_list - window_start]
    coarse_cols = up_equiv[:, coarse_list]
    gathered = jnp.einsum("ptf,tfc->cpt", far_cols, far_hot, precision=highest) + jnp.einsum(
        "ptf,tfc->cpt", coarse_cols, coarse_hot, precision=highest
    )
    down_check = jnp.einsum("cpq,cqt->pt", translations, gathered, precision=highest)
    down_equiv = jnp.dot(
        check_to_equiv, down_check, precision=highest, preferred_element_type=jnp.float32
    )
    surface = surface_points(ORDER)
    far_leaves = math.gcd(own_leaves, 16)
    far_blocks = own_leaves // far_leaves

    def far_step(inputs):
        local_pos, equiv_rows = inputs
        return far_block(local_pos, equiv_rows, surface)

    far_pot = lax.map(
        far_step,
        (
            sources[:, :3, :].reshape(far_blocks, far_leaves, 3, leaf_pts),
            down_equiv.T.reshape(far_blocks, far_leaves, -1),
        ),
    )
    far_pot = far_pot.reshape(own_leaves, leaf_pts)
    return jnp.where(is_live, near_pot + far_pot, 0.0)


def solution(mesh):
    return jax.shard_map(
        on_device,
        mesh=mesh,
        in_specs=(
            P(("gx", "gy"), None, None),
            P(("gx", "gy")),
            P(None, ("gx", "gy")),
            P(("gx", "gy"), None),
            P(("gx", "gy"), None),
            P(("gx", "gy"), None),
            P(("gx", "gy"), None),
            P(("gx", "gy"), None),
            P(),
            P(),
            P(),
            P(("gx", "gy"), None, None),
            P(("gx", "gy"), None),
        ),
        out_specs=P(("gx", "gy"), None),
        check_vma=False,
    )
```

profile of v0, /device:TPU:1, one launch (start us, length us, event | category | flops | bytes accessed | tf_op | source)
XLA Modules:
  0.0 323.7 jit_solution(13460825076215052948)
XLA Ops:
  6.5 5.2 %collective-permute-start.3 = (f32[296,32]{0,1:T(8,128)}, f32[296,32]{0,1:T(8,128)S(1)}, u32[]{:S(2)}, u32[]{:S(2)}) collective-permute-start(f32[296,32]{0,1:T(8,128)} %param.20), channel_id=1, source_target_pairs={{1,0},{2,1},{3,2},{4,3},{5,4},{6,5},{7,6},{8,7},{9,8},{10,9},{11,1... | collective-permute-start | bytes 113672 | tf_op jit(solution)/shard_map/ppermute | solution.py:26
  11.8 1.9 collective-permute-start.2
  13.8 0.9 slice.47
  14.7 1.0 broadcast_add_fusion
  15.7 0.7 copy_select_fusion
  16.5 2.4 collective-permute-start.1
  18.9 3.2 collective-permute-start
  22.0 2.7 convolution_bitcast_fusion.1
  24.7 0.7 compare_select_fusion.2
  25.6 0.7 compare_select_fusion.1
  26.5 0.7 broadcast_subtract_fusion
  27.2 0.8 copy.53
  27.9 0.8 copy.51
  28.8 0.8 pad_maximum_fusion.1
  29.6 1.6 gather_fusion.1
  31.5 22.2 %while.21 = (s32[]{:T(128)}, f32[4,8,256]{2,1,0:T(8,128)S(1)}, f32[4,8,3,256]{3,1,0,2:T(8,128)S(1)}, s32[4,8,4]{1,0,2:T(4,128)S(1)}, f32[96,4,256]{2,1,0:T(4,128)S(1)}, /*index=5*/s32[]{:T(128)}) while((s32[]{:T(128)}, f32[4,8,256]{2,1,0:T(8,128)S(1)}, f32[4,8,3,256]{3,1,0,2:T(8,128)S(1)}, s32[4,8,4]{1,0,2:T(4,128)S(1)}, ...), condition=%wide.region_2.3_spmd, body=%wide.region_0.2_spmd.sunk | while | flops 23067744 | bytes 1070425 | solution.py:122
  31.7 0.6 gather_fusion
  32.6 4.5 %multiply_reduce_fusion.2 = f32[8,256]{1,0:T(8,128)S(1)} fusion(f32[8,4,256]{2,1,0:T(4,128)S(1)} %get-tuple-element.209, f32[8,4,256]{2,1,0:T(4,128)S(1)} %get-tuple-element.210, f32[8,256]{1,0:T(8,128)S(1)} %get-tuple-element.211, f32[8,4,256]{2,1,0:T(4,128)S(1)} %get-tuple-element.214, f32[8,256]{1,0:T(8,128)S(1)} %get-tuple-element.215, ...), kind=kLoop, calls=%fused_computation.18.clone.1 | loop fusion | flops 23066624 | bytes 163840 | tf_op jit(solution)/shard_map/while/body/eval_jaxpr/reduce_sum | solution.py:61
  38.1 4.5 %multiply_reduce_fusion.2 = f32[8,256]{1,0:T(8,128)S(1)} fusion(f32[8,4,256]{2,1,0:T(4,128)S(1)} %get-tuple-element.209, f32[8,4,256]{2,1,0:T(4,128)S(1)} %get-tuple-element.210, f32[8,256]{1,0:T(8,128)S(1)} %get-tuple-element.211, f32[8,4,256]{2,1,0:T(4,128)S(1)} %get-tuple-element.214, f32[8,256]{1,0:T(8,128)S(1)} %get-tuple-element.215, ...), kind=kLoop, calls=%fused_computation.18.clone.1 | loop fusion | flops 23066624 | bytes 163840 | tf_op jit(solution)/shard_map/while/body/eval_jaxpr/reduce_sum | solution.py:61
  43.7 4.5 %multiply_reduce_fusion.2 = f32[8,256]{1,0:T(8,128)S(1)} fusion(f32[8,4,256]{2,1,0:T(4,128)S(1)} %get-tuple-element.209, f32[8,4,256]{2,1,0:T(4,128)S(1)} %get-tuple-element.210, f32[8,256]{1,0:T(8,128)S(1)} %get-tuple-element.211, f32[8,4,256]{2,1,0:T(4,128)S(1)} %get-tuple-element.214, f32[8,256]{1,0:T(8,128)S(1)} %get-tuple-element.215, ...), kind=kLoop, calls=%fused_computation.18.clone.1 | loop fusion | flops 23066624 | bytes 163840 | tf_op jit(solution)/shard_map/while/body/eval_jaxpr/reduce_sum | solution.py:61
  48.4 0.6 gather_fusion
  49.2 4.5 %multiply_reduce_fusion.2 = f32[8,256]{1,0:T(8,128)S(1)} fusion(f32[8,4,256]{2,1,0:T(4,128)S(1)} %get-tuple-element.209, f32[8,4,256]{2,1,0:T(4,128)S(1)} %get-tuple-element.210, f32[8,256]{1,0:T(8,128)S(1)} %get-tuple-element.211, f32[8,4,256]{2,1,0:T(4,128)S(1)} %get-tuple-element.214, f32[8,256]{1,0:T(8,128)S(1)} %get-tuple-element.215, ...), kind=kLoop, calls=%fused_computation.18.clone.1 | loop fusion | flops 23066624 | bytes 163840 | tf_op jit(solution)/shard_map/while/body/eval_jaxpr/reduce_sum | solution.py:61
  53.8 239.9 %all-reduce.2.cloned.1.call-done = f32[296,1024]{1,0:T(8,128)} async-done(((f32[296,1024]{1,0:T(8,128)}), f32[296,1024]{1,0:T(8,128)}) %all-reduce.2.cloned.1.call-update) | async-done | bytes 1212432 | tf_op jit(solution)/shard_map/psum | solution.py:110
  293.7 4.5 %convolution_bitcast_fusion = f32[296,1024]{1,0:T(8,128)} fusion(f32[296,1024]{1,0:T(8,128)} %all-reduce.2.cloned.1.call-done, f32[296,296]{1,0:T(8,128)S(1)} %copy-done), kind=kOutput, calls=%fused_computation.31 | convolution fusion | flops 1076625408 | bytes 2775296 | tf_op jit(solution)/shard_map/dot_general | solution.py:111
  298.2 1.7 copy.55
  299.9 1.0 gather_fusion.2
  300.9 0.7 fusion.8
  302.2 8.4 %convolution_bitcast_fusion.2 = f32[32,296]{1,0:T(8,128)S(1)} fusion(f32[16,296,296]{2,1,0:T(8,128)} %param.26, f32[16,296,32]{1,0,2:T(8,128)S(1)} %fusion.6), kind=kOutput, calls=%fused_computation.35 | convolution fusion | flops 538312704 | bytes 6251520 | tf_op jit(solution)/shard_map/cpq,cqt->pt/dot_general | solution.py:138
  311.2 5.0 %while.22 = (s32[]{:T(128)}, f32[2,16,256]{2,1,0:T(8,128)S(1)}, f32[2,16,3,256]{3,1,0,2:T(8,128)S(1)}, f32[2,16,296]{2,1,0:T(8,128)S(1)}, s32[]{:T(128)}, /*inde...) while((s32[]{:T(128)}, f32[2,16,256]{2,1,0:T(8,128)S(1)}, ...), condition=%wide.region_6.7_spmd.clone, body=%wide.region_4.6_spmd.sunk.clone.sunk | while | flops 13332482 | bytes 355401 | solution.py:150
  311.3 2.4 fusion.30
  313.8 2.4 fusion.30
  316.2 0.7 fusion.14
  (89 shorter events, 4.6 us)
Async XLA Ops:
  6.5 287.2 %copy-start = (f32[296,296]{1,0:T(8,128)S(1)}, f32[296,296]{1,0:T(8,128)}, u32[]{:S(2)}) copy-start(f32[296,296]{1,0:T(8,128)} %param.28) | copy-start | bytes 1051396
  6.5 287.1 %all-reduce.2.cloned.1.call-start = ((), (), s32[]{:S(2)}) async-start(), calls=%async_computation | async-start | bytes 2424832 | tf_op jit(solution)/shard_map/psum | solution.py:110
  6.5 22.2 %collective-permute-start.3 = (f32[296,32]{0,1:T(8,128)}, f32[296,32]{0,1:T(8,128)S(1)}, u32[]{:S(2)}, u32[]{:S(2)}) collective-permute-start(f32[296,32]{0,1:T(8,128)} %param.20), channel_id=1, source_target_pairs={{1,0},{2,1},{3,2},{4,3},{5,4},{6,5},{7,6},{8,7},{9,8},{10,9},{11,1... | collective-permute-start | bytes 113672 | tf_op jit(solution)/shard_map/ppermute | solution.py:26
  11.8 17.0 %collective-permute-start.2 = (f32[296,32]{0,1:T(8,128)}, f32[296,32]{0,1:T(8,128)S(1)}, u32[]{:S(2)}, u32[]{:S(2)}) collective-permute-start(f32[296,32]{0,1:T(8,128)} %param.20), channel_id=1, source_target_pairs={{0,1},{1,2},{2,3},{3,4},{4,5},{5,6},{6,7},{7,8},{8,9},{9,10},{10,1... | collective-permute-start | bytes 113672 | tf_op jit(solution)/shard_map/ppermute | solution.py:23
  16.5 14.8 %collective-permute-start.1 = (f32[32,4,256]{2,0,1:T(8,128)S(1)}, f32[32,4,256]{2,0,1:T(8,128)S(1)}, u32[]{:S(2)}, u32[]{:S(2)}) collective-permute-start(f32[32,4,256]{2,0,1:T(8,128)S(1)} %pad_maximum_fusion.2), channel_id=1, source_target_pairs={{1,0},{2,1},{3,2},{4,3},{5,4},{6,5},{7,6},{8,7},{9,8},{10,9},{11,1... | collective-permute-start | bytes 393224 | tf_op jit(solution)/shard_map/ppermute | solution.py:26
  18.9 12.4 %collective-permute-start = (f32[32,4,256]{2,0,1:T(8,128)S(1)}, f32[32,4,256]{2,0,1:T(8,128)S(1)}, u32[]{:S(2)}, u32[]{:S(2)}) collective-permute-start(f32[32,4,256]{2,0,1:T(8,128)S(1)} %pad_maximum_fusion.2), channel_id=1, source_target_pairs={{0,1},{1,2},{2,3},{3,4},{4,5},{5,6},{6,7},{7,8},{8,9},{9,10},{10,1... | collective-permute-start | bytes 393224 | tf_op jit(solution)/shard_map/ppermute | solution.py:23
  301.6 9.0 %copy-start.1 = (f32[296,296]{1,0:T(8,128)S(1)}, f32[296,296]{1,0:T(8,128)}, u32[]{:S(2)}) copy-start(f32[296,296]{1,0:T(8,128)} %param.27) | copy-start | bytes 1051396
  302.2 9.0 %copy-start.3 = (f32[296]{0:T(512)S(1)}, f32[296]{0:T(512)}, u32[]{:S(2)}) copy-start(f32[296]{0:T(512)} %constant.189) | copy-start | bytes 3556
  302.2 9.0 %copy-start.4 = (f32[296]{0:T(512)S(1)}, f32[296]{0:T(512)}, u32[]{:S(2)}) copy-start(f32[296]{0:T(512)} %constant.190) | copy-start | bytes 3556
  302.2 9.0 %copy-start.5 = (f32[296]{0:T(512)S(1)}, f32[296]{0:T(512)}, u32[]{:S(2)}) copy-start(f32[296]{0:T(512)} %constant.191) | copy-start | bytes 3556
  311.2 5.0 %copy-start.2 = (s32[32]{0:T(128)S(1)}, s32[32]{0:T(128)}, u32[]{:S(2)}) copy-start(s32[32]{0:T(128)} %param.19) | copy-start | bytes 388
Sparse Core Ops, SparseCore 0:
  24.8 268.7 all-reduce.1
where the time goes:
time: 326 us; the launch traced here: 324 us
  waiting for transfers between devices  240 us (74%)
  other arithmetic  28.3 us (9%)
  matrix products  17.3 us (5%)
  between operations  13.6 us (4%)
  starting transfers between devices  12.7 us (4%)
  local copies, waits for them, and re-layouts  11.4 us (3%)
    psum x1, waiting for transfers between devices, on_device(): up_check = lax.psum(local_dense, ('gx', 'gy'))  240 us
    reduce_sum x4, other arithmetic, near_block(): return jnp.sum(kernel * neighbours[:, :, 3, None, :], axis=(1, 3))  18 us
    dot_general x1, matrix products, on_device(): jnp.einsum('cpq,cqt->pt', translations, gathered, precision=highest)  8.4 us
    ppermute x2, starting transfers between devices, extended(): lax.ppermute(lax.slice_in_dim(block, 0, width, axis=dim), axis, backward)  7.63 us
  transfers between devices with their start and end apart: 5, of which 1 were waited for; matrix products, arithmetic and copies ran while one was open for 11% of the time, Pallas kernels for 0%

commit v1 on v0

--- a/solution.py
+++ b/solution.py
@@ -4,6 +4,8 @@
 import jax.numpy as jnp
 import numpy as np
 from jax import lax
+from jax.experimental import pallas as pl
+from jax.experimental.pallas import tpu as pltpu
 from jax.sharding import PartitionSpec as P
 
 ORDER = 8
@@ -13,19 +15,6 @@
 soft_sq = 0.0625
 surface_half = 2.5
 grid_side = 32
-
-
-def extended(block, sides, width):
-    for axis, dim in sides:
-        count = lax.axis_size(axis)
-        forward = [(i, i + 1) for i in range(count - 1)]
-        backward = [(target, source) for source, target in forward]
-        low = lax.ppermute(
-            lax.slice_in_dim(block, block.shape[dim] - width, None, axis=dim), axis, forward
-        )
-        high = lax.ppermute(lax.slice_in_dim(block, 0, width, axis=dim), axis, backward)
-        block = jnp.concatenate([low, block, high], axis=dim)
-    return block
 
 
 def surface_points(surf_order):
@@ -69,6 +58,151 @@
         gap_first * gap_first + gap_second * gap_second + gap_third * gap_third + soft_sq
     )
     return jnp.sum(kernel * equiv_rows[:, None, :], axis=2)
+
+
+MESH = pl.DeviceIdType.MESH
+
+
+def up_kernel(ids_ref, part_ref, mat_ref, dens_ref, pack_ref, pv_ref, dw_ref, sw_ref, wt, rt, p0s, p0r, hs, hr, zs, zr, as_, ar, bs, br, fs, fr):
+    highest = lax.Precision.HIGHEST
+    z = lax.axis_index("gx")
+    gy = lax.axis_index("gy")
+    x, y, c = gy // 8, (gy // 2) % 4, gy % 2
+    chip = z * 16 + x * 4 + y
+    partner = (z, gy + 1 - 2 * c)
+    a = x + c * (y - x)
+    b = y + c * (x - y)
+
+    def chip_dev(q, core):
+        return (q // 16, ((q // 4) % 4) * 8 + (q % 4) * 2 + core)
+
+    def ab_dev(a1, b1):
+        return (z, (a1 + c * (b1 - a1)) * 8 + (b1 + c * (a1 - b1)) * 2 + c)
+
+    prev_chip = (chip + 127) % 128
+    next_chip = (chip + 1) % 128
+    adj_chip = (chip + 127 + 2 * c) % 128
+
+    barrier = pltpu.get_barrier_semaphore()
+    peers = [partner, chip_dev(prev_chip, 1), chip_dev(next_chip, 0)]
+    peers += [((z + k) % 8, gy) for k in range(1, 8)]
+    peers += [ab_dev((a + k) % 4, b) for k in range(1, 4)]
+    peers += [ab_dev(a, (b + k) % 4) for k in range(1, 4)]
+    for peer in peers:
+        pl.semaphore_signal(barrier, inc=1, device_id=peer, device_id_type=MESH)
+
+    rows = lax.broadcasted_iota(jnp.int32, (16, 64), 0)
+    adj_base = 8 * chip - 8 + 16 * c
+    wanted = jnp.where(rows < 8, 8 * chip + rows, adj_base + rows - 8)
+    hot = (wanted == ids_ref[...]).astype(jnp.float32)
+    mine = jnp.dot(hot, part_ref[...], precision=highest, preferred_element_type=jnp.float32)
+    mine = lax.dot_general(mine, mat_ref[...], (((1,), (1,)), ((), ())), precision=highest, preferred_element_type=jnp.float32)
+    wt[...] = jnp.zeros_like(wt)
+    wt[0, :, 0:296] = mine[0:8]
+    wt[1, :, 0:296] = mine[8:16]
+
+    pl.semaphore_wait(barrier, len(peers))
+
+    def rcopy(src, dst, ssem, rsem, dev):
+        return pltpu.make_async_remote_copy(src_ref=src, dst_ref=dst, send_sem=ssem, recv_sem=rsem, device_id=dev, device_id_type=MESH)
+
+    sends = []
+
+    def send(src, dst, ssem, rsem, dev):
+        cp = rcopy(src, dst, ssem, rsem, dev)
+        cp.start()
+        sends.append(cp)
+
+    send(wt.at[1], rt.at[2 - c], p0s.at[1], p0r.at[2 - c], chip_dev(adj_chip, 0))
+    send(wt.at[1], rt.at[2 - c], p0s.at[2], p0r.at[2 - c], chip_dev(adj_chip, 1))
+    send(wt.at[0], rt.at[0], p0s.at[0], p0r.at[0], partner)
+    d = z * 32 + gy
+    up_d, down_d = (d + 1) % 256, (d + 255) % 256
+    up_dev, down_dev = (up_d // 32, up_d % 32), (down_d // 32, down_d % 32)
+    send(pack_ref, sw_ref.at[0], hs.at[0], hr.at[0], up_dev)
+    send(pack_ref, sw_ref.at[1], hs.at[1], hr.at[1], down_dev)
+    send(dens_ref, dw_ref.at[0], hs.at[2], hr.at[2], up_dev)
+    send(dens_ref, dw_ref.at[1], hs.at[3], hr.at[3], down_dev)
+
+    def arrive(dst, rsem):
+        rcopy(dst, dst, fs.at[0], rsem, partner).wait_recv()
+
+    for k in range(3):
+        arrive(rt.at[k], p0r.at[k])
+    total = wt[0] + rt[0] + rt[1] + rt[2]
+    tile = jnp.where(c == 0, total[:, 0:128], total[:, 128:256])
+    tail = jnp.where(c == 0, total[0:4, 256:384], total[4:8, 256:384])
+    pv_ref[c, b, a, z, 0] = tile[0:4]
+    pv_ref[c, b, a, z, 1] = tile[4:8]
+    pv_ref[c, b, a, z, 2] = tail
+
+    for k in (4, 3, 5, 2, 6, 1, 7):
+        spot = pv_ref.at[c, b, a, z]
+        send(spot, spot, zs.at[k - 1], zr.at[k - 1], ((z + k) % 8, gy))
+    for k in (1, 7, 2, 6, 3, 5, 4):
+        arrive(pv_ref.at[c, b, a, (z + 8 - k) % 8], zr.at[k - 1])
+
+    forwards = 0
+
+    def forward(spot):
+        nonlocal forwards
+        send(spot, spot, fs.at[forwards], fr.at[forwards], partner)
+        forwards += 1
+
+    spot = pv_ref.at[c, b, a]
+    for k in (2, 1, 3):
+        send(spot, spot, as_.at[k - 1], ar.at[k - 1], ab_dev((a + k) % 4, b))
+    for k in (2, 1, 3):
+        send(spot, spot, bs.at[0, k - 1], br.at[0, k - 1], ab_dev(a, (b + k) % 4))
+    forward(spot)
+    for j in (1, 3, 2):
+        spot = pv_ref.at[c, b, (a + 4 - j) % 4]
+        arrive(spot, ar.at[j - 1])
+        for k in (2, 1, 3):
+            send(spot, spot, bs.at[j, k - 1], br.at[j, k - 1], ab_dev(a, (b + k) % 4))
+        forward(spot)
+    for j in (0, 1, 3, 2):
+        for k in (1, 3, 2):
+            spot = pv_ref.at[c, (b + 4 - k) % 4, (a + 4 - j) % 4]
+            arrive(spot, br.at[j, k - 1])
+            forward(spot)
+    n = 0
+    arrive(pv_ref.at[1 - c, a, b], fr.at[n])
+    n += 1
+    for j in (1, 3, 2):
+        arrive(pv_ref.at[1 - c, a, (b + 4 - j) % 4], fr.at[n])
+        n += 1
+    for j in (0, 1, 3, 2):
+        for k in (1, 3, 2):
+            arrive(pv_ref.at[1 - c, (a + 4 - k) % 4, (b + 4 - j) % 4], fr.at[n])
+            n += 1
+    for k in range(2):
+        arrive(sw_ref.at[k], hr.at[k])
+        arrive(dw_ref.at[k], hr.at[2 + k])
+    for cp in sends:
+        cp.wait_send()
+
+
+def exchange(contrib_ids, partial_t, up_matrix, dens_t, packed):
+    vmem = pl.BlockSpec(memory_space=pltpu.VMEM)
+    dma = pltpu.SemaphoreType.DMA
+    return pl.pallas_call(
+        up_kernel,
+        out_shape=(
+            jax.ShapeDtypeStruct((2, 4, 4, 8, 3, 4, 128), jnp.float32),
+            jax.ShapeDtypeStruct((2, 32, 296), jnp.float32),
+            jax.ShapeDtypeStruct((2, 32, 4, 256), jnp.float32),
+        ),
+        in_specs=[vmem] * 5,
+        out_specs=(vmem, vmem, vmem),
+        scratch_shapes=[
+            pltpu.VMEM((2, 8, 384), jnp.float32),
+            pltpu.VMEM((3, 8, 384), jnp.float32),
+            dma((3,)), dma((3,)), dma((4,)), dma((4,)), dma((7,)), dma((7,)),
+            dma((3,)), dma((3,)), dma((4, 3)), dma((4, 3)), dma((16,)), dma((16,)),
+        ],
+        compiler_params=pltpu.CompilerParams(collective_id=0, has_side_effects=True),
+    )(contrib_ids, partial_t, up_matrix, dens_t, packed)
 
 
 def on_device(
@@ -98,19 +232,20 @@
     positions = sources[:, :3, :] + centres[:, :, None]
     charges = jnp.where(is_live, sources[:, 3, :], 0.0)
     packed = jnp.concatenate([positions, charges[:, None, :]], axis=1)
-    window = extended(packed, ((("gx", "gy"), 0),), own_leaves)
-    dens_window = extended(densities, ((("gx", "gy"), 1),), own_leaves)
-    partial_value = partial_check[0]
-    slot_ids = contrib_ids[0]
-    octant_ids = jnp.arange(SHARED, dtype=jnp.int32)
-    spread_hot = (slot_ids[:, None] == octant_ids[None, :]).astype(jnp.float32)
-    local_dense = jnp.dot(
-        partial_value, spread_hot, precision=highest, preferred_element_type=jnp.float32
-    )
-    up_check = lax.psum(local_dense, ("gx", "gy"))
-    up_equiv = jnp.dot(
-        up_check_to_equiv, up_check, precision=highest, preferred_element_type=jnp.float32
-    )
+    dens_t = densities.T
+    pieces, dens_sides, near_sides = exchange(
+        contrib_ids, partial_check[0].T, up_check_to_equiv, dens_t, packed
+    )
+    window = jnp.concatenate([near_sides[0], packed, near_sides[1]], axis=0)
+    dens_window = jnp.concatenate([dens_sides[0], dens_t, dens_sides[1]], axis=0).T
+    first = pieces[0]
+    second = pieces[1].transpose(1, 0, 2, 3, 4, 5)
+    block_a = first[:, :, :, 0:2].reshape(4, 4, 8, 8, 128)
+    block_b = second[:, :, :, 0:2].reshape(4, 4, 8, 8, 128)
+    block_c = jnp.concatenate([first[:, :, :, 2], second[:, :, :, 2]], axis=3)
+    up_rows = jnp.concatenate([block_a, block_b, block_c], axis=4)
+    up_rows = up_rows.transpose(2, 1, 0, 3, 4).reshape(SHARED, 384)[:, :296]
+    up_equiv = up_rows.T
     near_local = near_list - window_start
     step_leaves = math.gcd(own_leaves, 8)
     blocks = own_leaves // step_leaves

time: 326 us -> 85.1 us (0.26)
  waiting for transfers between devices: 240 us -> 0 us
  Pallas kernels: 0 us -> 35 us
  between operations: 13.6 us -> 0.37 us
  starting transfers between devices: 12.7 us -> 0 us
  matrix products: 17.3 us -> 10.2 us
    psum x1 -> x0, waiting for transfers between devices: 240 us -> none  [on_device(): up_check = lax.psum(local_dense, ('gx', 'gy'))]
    pallas_call x0 -> x1, Pallas kernels: none -> 35 us  [exchange(): pl.pallas_call(up_kernel, out_shape=(jax.ShapeDtypeStruct((2, 4, 4, 8, 3,...]
    ppermute x4 -> x0, starting transfers between devices: 12.7 us -> none  [the longest x2 7.63 us: extended(): lax.ppermute(lax.slice_in_dim(block, 0, width, axis=dim), axis, backward)]
    dot_general x2 -> x0, matrix products: 7.14 us -> none  [the longest x1 4.47 us: on_device(): jnp.dot(up_check_to_equiv, up_check, precision=highest, preferred_element...]
  transfers between devices with their start and end apart: 5 -> 0, of which waited for: 1 -> 0; matrix products, arithmetic and copies ran while one was open for 11% -> 0% of each run, Pallas kernels for 0% -> 0%
where the time goes in v1:
time: 85.1 us; the launch traced here: 84.8 us
  Pallas kernels  35 us (41%)
  other arithmetic  27.4 us (32%)
  local copies, waits for them, and re-layouts  11.4 us (13%)
  matrix products  10.2 us (12%)
    pallas_call x1, Pallas kernels, exchange(): pl.pallas_call(up_kernel, out_shape=(jax.ShapeDtypeStruct((2, 4, 4, 8, 3,...  35 us
    reduce_sum x4, other arithmetic, near_block(): return jnp.sum(kernel * neighbours[:, :, 3, None, :], axis=(1, 3))  18 us
    dot_general x1, matrix products, on_device(): jnp.einsum('cpq,cqt->pt', translations, gathered, precision=highest)  8.4 us
    reduce_sum x2, other arithmetic, far_block(): return jnp.sum(kernel * equiv_rows[:, None, :], axis=2)  4.83 us
    gather x4, local copies, waits for them, and re-layouts, near_step(): return near_block(targets, window[chosen])  2.53 us

profile of v1, /device:TPU:1, one launch (start us, length us, event | category | flops | bytes accessed | tf_op | source)
XLA Modules:
  0.0 84.8 jit_solution(6137757697956189645)
XLA Ops:
  0.1 1.0 %broadcast_add_fusion = (f32[32,3,256]{2,1,0:T(4,128)S(1)}, f32[32,3,256]{2,1,0:T(4,128)S(1)}) fusion(f32[32,3]{1,0:T(8,128)S(1)} %copy.42, f32[32,4,256]{2,1,0:T(4,128)} %param.18), kind=kLoop, calls=%fused_computation.53 | loop fusion | flops 24576 | bytes 295296 | tf_op jit(solution)/shard_map/add | solution.py:232
  1.2 1.0 %compare_select_fusion.1 = f32[32,1,256]{2,1,0:T(1,128)S(1)} fusion(f32[32,4,256]{2,1,0:T(4,128)} %param.18, s32[32]{0:T(128)} %param.19), kind=kLoop, calls=%fused_computation.51 | loop fusion | flops 16384 | bytes 65664 | tf_op jit(solution)/shard_map/jit(_where)/select_n | solution.py:233
  2.2 0.7 pad_maximum_fusion.1.pack_ref
  2.9 35.0 %shard_map.136 = (f32[2,4,4,8,3,4,128]{6,5,4,3,2,1,0:T(4,128)}, f32[2,32,296]{2,1,0:T(8,128)}, f32[2,32,4,256]{3,2,1,0:T(4,128)}) custom-call(s32[1,64]{1,0:T(1,128)} %ids_ref.1, f32[64,296]{1,0:T(8,128)} %bitcast.127, f32[296,296]{1,0:T(8,128)} %mat_ref.1, f32[32,296]{1,0:T(8,128)} %bitcast.125, f32[32,4,256]{2,1,0:T(4,128)} %pad_maximum_fusion.1.pack_ref), custom_call_target="tpu_custom_call" | custom-call | tf_op jit(solution)/shard_map/pallas_call | solution.py:189
  37.9 1.2 %slice_bitcast_fusion.8 = f32[4,4,8,3,4,128]{5,4,3,2,0,1:T(4,128)S(1)} fusion(f32[2,4,4,8,3,4,128]{6,5,4,3,2,1,0:T(4,128)} %get-tuple-element.65), kind=kLoop, calls=%fused_computation.38 | loop fusion | bytes 1572864 | tf_op jit(solution)/shard_map/transpose | solution.py:242
  39.2 1.3 %slice_bitcast_fusion.7 = f32[4,4,8,3,4,128]{5,4,2,0,1,3:T(4,128)S(1)} fusion(f32[2,4,4,8,3,4,128]{6,5,4,3,2,1,0:T(4,128)} %get-tuple-element.65), kind=kLoop, calls=%fused_computation.36 | loop fusion | bytes 1572864 | tf_op jit(solution)/shard_map/squeeze | solution.py:241
  40.8 0.2 maximum_bitcast_fusion
  41.0 0.2 copy.50
  41.2 0.1 slice_bitcast_fusion.6
  41.3 0.2 copy-done.5
  41.7 1.0 %gather_fusion.2 = f32[256,296]{1,0:T(8,128)S(1)} fusion(f32[296,1024]{0,1:T(8,128)S(1)} %slice_bitcast_fusion.6, s32[1024]{0:T(1024)S(1)} %pad_clamp_fusion.1), kind=kCustom, calls=%fused_computation.2 | custom fusion | bytes 607232 | tf_op jit(solution)/shard_map/gather | solution.py:269
  42.8 0.7 fusion.8
  43.5 0.8 slice_bitcast_fusion.14
  44.3 0.7 compare_select_fusion.2
  45.2 1.6 %gather_fusion.1 = f32[512,296]{1,0:T(8,128)S(1)} fusion(f32[296,96]{0,1:T(8,128)S(1)} %maximum_bitcast_fusion.1, s32[1024]{0:T(1024)S(1)} %pad_clamp_fusion.2), kind=kCustom, calls=%fused_computation.1 | custom fusion | bytes 1214464 | tf_op jit(solution)/shard_map/gather | solution.py:268
  46.9 0.6 fusion.6
  47.5 8.4 %convolution_bitcast_fusion = f32[32,296]{1,0:T(8,128)S(1)} fusion(f32[16,296,296]{2,1,0:T(8,128)} %param.26, f32[16,296,32]{1,0,2:T(8,128)S(1)} %fusion.6), kind=kOutput, calls=%fused_computation.35 | convolution fusion | flops 538312704 | bytes 6251520 | tf_op jit(solution)/shard_map/cpq,cqt->pt/dot_general | solution.py:273
  55.9 0.5 fusion.18
  56.5 5.0 %while.22 = (s32[]{:T(128)}, f32[2,16,256]{2,1,0:T(8,128)S(1)}, f32[2,16,3,256]{3,1,2,0:T(8,128)S(1)}, f32[2,16,296]{2,1,0:T(8,128)S(1)}, s32[]{:T(128)}, /*inde...) while((s32[]{:T(128)}, f32[2,16,256]{2,1,0:T(8,128)S(1)}, ...), condition=%wide.region_5.6_spmd.clone, body=%wide.region_3.5_spmd.sunk.clone.sunk | while | flops 13332482 | bytes 355401 | solution.py:285
  56.6 2.4 %fusion.27 = f32[16,256]{1,0:T(8,128)S(1)} fusion(f32[296]{0:T(512)S(1)} %get-tuple-element.251, f32[296]{0:T(512)S(1)} %get-tuple-element.252, f32[296]{0:T(512)S(1)} %get-tuple-element.253, f32[16,296]{1,0:T(8,128)S(1)} %dynamic-slice_bitcast_fusion.7, f32[16,256]{1,0:T(8,128)S(1)} %get-tuple-element.227, f32[16,256]{1,0:T(8,128)S(1)} %get-tuple-element.228, ...), kind=kLoop, calls=%fused_computation.8.clone.1 | loop fusion | flops 13332480 | bytes 88032 | tf_op jit(solution)/shard_map/while/body/eval_jaxpr/reduce_sum | solution.py:60
  59.1 2.4 %fusion.27 = f32[16,256]{1,0:T(8,128)S(1)} fusion(f32[296]{0:T(512)S(1)} %get-tuple-element.251, f32[296]{0:T(512)S(1)} %get-tuple-element.252, f32[296]{0:T(512)S(1)} %get-tuple-element.253, f32[16,296]{1,0:T(8,128)S(1)} %dynamic-slice_bitcast_fusion.7, f32[16,256]{1,0:T(8,128)S(1)} %get-tuple-element.227, f32[16,256]{1,0:T(8,128)S(1)} %get-tuple-element.228, ...), kind=kLoop, calls=%fused_computation.8.clone.1 | loop fusion | flops 13332480 | bytes 88032 | tf_op jit(solution)/shard_map/while/body/eval_jaxpr/reduce_sum | solution.py:60
  61.7 0.1 pad_maximum_fusion
  61.8 22.3 %while.21 = (s32[]{:T(128)}, f32[4,8,256]{2,1,0:T(8,128)S(1)}, f32[4,8,3,256]{3,1,2,0:T(8,128)S(1)}, s32[4,8,4]{1,0,2:T(4,128)S(1)}, f32[96,4,256]{2,1,0:T(4,128)S(1)}, /*index=5*/s32[]{:T(128)}) while((s32[]{:T(128)}, f32[4,8,256]{2,1,0:T(8,128)S(1)}, f32[4,8,3,256]{3,1,2,0:T(8,128)S(1)}, s32[4,8,4]{1,0,2:T(4,128)S(1)}, ...), condition=%wide.region_2.3_spmd, body=%wide.region_0.2_spmd.sunk | while | flops 23067744 | bytes 1070425 | solution.py:257
  62.0 0.6 gather_fusion
  62.9 4.5 %multiply_reduce_fusion.2 = f32[8,256]{1,0:T(8,128)S(1)} fusion(f32[8,4,256]{2,1,0:T(4,128)S(1)} %get-tuple-element.214, f32[8,4,256]{2,1,0:T(4,128)S(1)} %get-tuple-element.215, f32[8,256]{1,0:T(8,128)S(1)} %get-tuple-element.216, f32[8,4,256]{2,1,0:T(4,128)S(1)} %get-tuple-element.219, f32[8,256]{1,0:T(8,128)S(1)} %get-tuple-element.220, ...), kind=kLoop, calls=%fused_computation.18.clone.1 | loop fusion | flops 23066624 | bytes 163840 | tf_op jit(solution)/shard_map/while/body/eval_jaxpr/reduce_sum | solution.py:50
  67.6 0.6 gather_fusion
  68.4 4.5 %multiply_reduce_fusion.2 = f32[8,256]{1,0:T(8,128)S(1)} fusion(f32[8,4,256]{2,1,0:T(4,128)S(1)} %get-tuple-element.214, f32[8,4,256]{2,1,0:T(4,128)S(1)} %get-tuple-element.215, f32[8,256]{1,0:T(8,128)S(1)} %get-tuple-element.216, f32[8,4,256]{2,1,0:T(4,128)S(1)} %get-tuple-element.219, f32[8,256]{1,0:T(8,128)S(1)} %get-tuple-element.220, ...), kind=kLoop, calls=%fused_computation.18.clone.1 | loop fusion | flops 23066624 | bytes 163840 | tf_op jit(solution)/shard_map/while/body/eval_jaxpr/reduce_sum | solution.py:50
  73.2 0.6 gather_fusion
  74.0 4.5 %multiply_reduce_fusion.2 = f32[8,256]{1,0:T(8,128)S(1)} fusion(f32[8,4,256]{2,1,0:T(4,128)S(1)} %get-tuple-element.214, f32[8,4,256]{2,1,0:T(4,128)S(1)} %get-tuple-element.215, f32[8,256]{1,0:T(8,128)S(1)} %get-tuple-element.216, f32[8,4,256]{2,1,0:T(4,128)S(1)} %get-tuple-element.219, f32[8,256]{1,0:T(8,128)S(1)} %get-tuple-element.220, ...), kind=kLoop, calls=%fused_computation.18.clone.1 | loop fusion | flops 23066624 | bytes 163840 | tf_op jit(solution)/shard_map/while/body/eval_jaxpr/reduce_sum | solution.py:50
  78.7 0.6 gather_fusion
  79.5 4.5 %multiply_reduce_fusion.2 = f32[8,256]{1,0:T(8,128)S(1)} fusion(f32[8,4,256]{2,1,0:T(4,128)S(1)} %get-tuple-element.214, f32[8,4,256]{2,1,0:T(4,128)S(1)} %get-tuple-element.215, f32[8,256]{1,0:T(8,128)S(1)} %get-tuple-element.216, f32[8,4,256]{2,1,0:T(4,128)S(1)} %get-tuple-element.219, f32[8,256]{1,0:T(8,128)S(1)} %get-tuple-element.220, ...), kind=kLoop, calls=%fused_computation.18.clone.1 | loop fusion | flops 23066624 | bytes 163840 | tf_op jit(solution)/shard_map/while/body/eval_jaxpr/reduce_sum | solution.py:50
  84.1 0.7 fusion.12
  (99 shorter events, 2.5 us)
Async XLA Ops:
  0.0 55.9 %copy-start = (f32[296,296]{1,0:T(8,128)S(1)}, f32[296,296]{1,0:T(8,128)}, u32[]{:S(2)}) copy-start(f32[296,296]{1,0:T(8,128)} %param.27) | copy-start | bytes 1051396
  40.8 0.7 copy-start.5
  41.7 1.0 %copy-start.4 = (s32[32,8]{0,1:T(8,128)S(1)}, s32[32,8]{0,1:T(8,128)}, u32[]{:S(2)}) copy-start(s32[32,8]{0,1:T(8,128)} %param.25) | copy-start | bytes 3076
  41.7 2.6 %copy-start.2 = (f32[296,32]{0,1:T(8,128)S(1)}, f32[296,32]{0,1:T(8,128)}, u32[]{:S(2)}) copy-start(f32[296,32]{0,1:T(8,128)} %param.20) | copy-start | bytes 113668
  45.2 1.6 %copy-start.3 = (s32[32,16]{0,1:T(8,128)S(1)}, s32[32,16]{0,1:T(8,128)}, u32[]{:S(2)}) copy-start(s32[32,16]{0,1:T(8,128)} %param.23) | copy-start | bytes 6148
  47.5 9.0 %copy-start.8 = (f32[296]{0:T(512)S(1)}, f32[296]{0:T(512)}, u32[]{:S(2)}) copy-start(f32[296]{0:T(512)} %constant.189) | copy-start | bytes 3556
  47.5 9.0 %copy-start.9 = (f32[296]{0:T(512)S(1)}, f32[296]{0:T(512)}, u32[]{:S(2)}) copy-start(f32[296]{0:T(512)} %constant.190) | copy-start | bytes 3556
  47.5 9.0 %copy-start.10 = (f32[296]{0:T(512)S(1)}, f32[296]{0:T(512)}, u32[]{:S(2)}) copy-start(f32[296]{0:T(512)} %constant.191) | copy-start | bytes 3556
  56.5 5.1 %copy-start.7 = (s32[32,4]{0,1:T(4,128)S(1)}, s32[32,4]{0,1:T(4,128)}, u32[]{:S(2)}) copy-start(s32[32,4]{0,1:T(4,128)} %param.21) | copy-start | bytes 1540
  56.5 5.2 %copy-start.1 = (f32[2,32,4,256]{3,2,1,0:T(4,128)S(1)}, f32[2,32,4,256]{3,2,1,0:T(4,128)}, u32[]{:S(2)}) copy-start(f32[2,32,4,256]{3,2,1,0:T(4,128)} %get-tuple-element.62) | copy-start | bytes 786436
  61.8 22.3 %copy-start.6 = (s32[32]{0:T(128)S(1)}, s32[32]{0:T(128)}, u32[]{:S(2)}) copy-start(s32[32]{0:T(128)} %param.19) | copy-start | bytes 388

commit v2 on v1

v2 whole, which is shorter than its diff:
```python
import jax
import jax.numpy as jnp
import numpy as np
from jax import lax
from jax.experimental import pallas as pl
from jax.experimental.pallas import tpu as pltpu
from jax.sharding import PartitionSpec as P

MESH = pl.DeviceIdType.MESH
ORDER = 8
P_SIZE = 296
SOFT = 0.0625
HALF = 2.5
PARTS = 48
NEAR_SPLIT = (0, 8, 14, 32, 32)


def surface_rows():
    ladder = np.arange(ORDER)
    grid = np.stack(np.meshgrid(ladder, ladder, ladder, indexing="ij")).reshape(3, -1)
    grid = grid[:, ((grid == 0) | (grid == ORDER - 1)).any(axis=0)].astype(np.float32)
    return (-HALF + 2.0 * HALF * grid / (ORDER - 1)).astype(np.float32)


def two(v):
    high = v.astype(jnp.bfloat16).astype(jnp.float32)
    low = (v - high).astype(jnp.bfloat16).astype(jnp.float32)
    return high, low


def three(v):
    high, mid = two(v)
    return high, mid, (v - high - mid).astype(jnp.bfloat16).astype(jnp.float32)


def target_rows(v):
    high, low = two(v)
    seen = high + low
    one = jnp.ones_like(v)
    return (high, high, low, low, one, one, one) + three(seen * seen)


def source_rows(v):
    high, low = two(v)
    seen = high + low
    one = jnp.ones_like(v)
    return (-2.0 * high, -2.0 * low, -2.0 * high, -2.0 * low) + three(seen * seen) + (one, one, one)


def dot_t(a, b):
    return lax.dot_general(a, b, (((1,), (1,)), ((), ())), preferred_element_type=jnp.float32)


def dot_n(a, b):
    return jnp.dot(a, b, preferred_element_type=jnp.float32)


def halves(v):
    high = v.astype(jnp.bfloat16)
    return high, (v - high.astype(jnp.float32)).astype(jnp.bfloat16)


def fmm_kernel(
    near_ref, live_ref, src_hbm, dens_hbm, flist_hbm, fclass_hbm, clist_hbm, cclass_hbm, trans_hbm, down_hbm, up_hbm,
    part_hbm, ids_hbm, surf_hbm, out_ref,
    pv_ref, wt, rt, win, dw, flist, fclass, clist, cclass, trans, down, up, part, ids, surf,
    tfeat, fa, fb, qa, qb, th, tl, gfar, up_high, up_low, equiv, near_rows,
    p0s, p0r, hs, hr, zs, zr, as_, ar, bs, br, fs, fr, ls,
):
    highest = lax.Precision.HIGHEST
    z = lax.axis_index("gx")
    gy = lax.axis_index("gy")
    x, y, c = gy // 8, (gy // 2) % 4, gy % 2
    chip = z * 16 + x * 4 + y
    d = z * 32 + gy
    partner = (z, gy + 1 - 2 * c)
    a = x + c * (y - x)
    b = y + c * (x - y)

    def chip_dev(q, core):
        return (q // 16, ((q // 4) % 4) * 8 + (q % 4) * 2 + core)

    def ab_dev(a1, b1):
        return (z, (a1 + c * (b1 - a1)) * 8 + (b1 + c * (a1 - b1)) * 2 + c)

    prev_chip = (chip + 127) % 128
    next_chip = (chip + 1) % 128
    adj_chip = (chip + 127 + 2 * c) % 128

    barrier = pltpu.get_barrier_semaphore()
    peers = [partner, chip_dev(prev_chip, 1), chip_dev(next_chip, 0)]
    peers += [((z + k) % 8, gy) for k in (4, 3, 5, 2, 6, 1, 7)]
    peers += [ab_dev((a + k) % 4, b) for k in range(1, 4)]
    peers += [ab_dev(a, (b + k) % 4) for k in range(1, 4)]
    for peer in peers:
        pl.semaphore_signal(barrier, inc=1, device_id=peer, device_id_type=MESH)

    loads = [
        pltpu.make_async_copy(s, t, ls.at[i])
        for i, (s, t) in enumerate(
            (
                (ids_hbm, ids), (part_hbm, part), (up_hbm, up), (src_hbm, win.at[pl.ds(32, 32)]),
                (dens_hbm, dw.at[pl.ds(32, 32)]), (flist_hbm, flist), (fclass_hbm, fclass), (clist_hbm, clist),
                (cclass_hbm, cclass), (surf_hbm, surf), (down_hbm, down), (trans_hbm, trans),
            )
        )
    ]
    for load in loads:
        load.start()

    rows = lax.broadcasted_iota(jnp.int32, (16, 64), 0)
    adj_base = 8 * chip - 8 + 16 * c
    wanted = jnp.where(rows < 8, 8 * chip + rows, adj_base + rows - 8)
    wt[...] = jnp.zeros_like(wt)
    for load in loads[0:3]:
        load.wait()
    hot = (wanted == ids[...]).astype(jnp.float32)
    mine = jnp.dot(hot, part[...], precision=highest, preferred_element_type=jnp.float32)
    mine = lax.dot_general(
        mine, up[...], (((1,), (1,)), ((), ())), precision=highest, preferred_element_type=jnp.float32
    )
    wt[0, :, 0:P_SIZE] = mine[0:8]
    wt[1, :, 0:P_SIZE] = mine[8:16]
    loads[3].wait()
    spot_row = lax.broadcasted_iota(jnp.int32, (4, 256), 0)
    spot_lane = lax.broadcasted_iota(jnp.int32, (4, 256), 1)

    def mask_leaf(t, carry):
        v = win[32 + t]
        win[32 + t] = jnp.where((spot_row == 3) & (spot_lane >= live_ref[t]), 0.0, v)
        return carry

    lax.fori_loop(0, 32, mask_leaf, 0)

    pl.semaphore_wait(barrier, len(peers))

    def rcopy(src, dst, ssem, rsem, dev):
        return pltpu.make_async_remote_copy(
            src_ref=src, dst_ref=dst, send_sem=ssem, recv_sem=rsem, device_id=dev, device_id_type=MESH
        )

    sends = []

    def send(src, dst, ssem, rsem, dev):
        cp = rcopy(src, dst, ssem, rsem, dev)
        cp.start()
        sends.append(cp)

    def arrive(dst, rsem):
        rcopy(dst, dst, fs.at[0], rsem, partner).wait_recv()

    send(wt.at[1], rt.at[2 - c], p0s.at[1], p0r.at[2 - c], chip_dev(adj_chip, 0))
    send(wt.at[1], rt.at[2 - c], p0s.at[2], p0r.at[2 - c], chip_dev(adj_chip, 1))
    send(wt.at[0], rt.at[0], p0s.at[0], p0r.at[0], partner)
    up_d, down_d = (d + 1) % 256, (d + 255) % 256
    up_dev, down_dev = (up_d // 32, up_d % 32), (down_d // 32, down_d % 32)
    own = win.at[pl.ds(32, 32)]
    send(own, win.at[pl.ds(0, 32)], hs.at[0], hr.at[0], up_dev)
    send(own, win.at[pl.ds(64, 32)], hs.at[1], hr.at[1], down_dev)
    send(dens_hbm, dw.at[pl.ds(0, 32)], hs.at[2], hr.at[2], up_dev)
    send(dens_hbm, dw.at[pl.ds(64, 32)], hs.at[3], hr.at[3], down_dev)

    def target_step(t, carry):
        v = jnp.where(spot_row < 3, win[32 + t], 0.0)
        for i, piece in enumerate(target_rows(v)):
            fa[4 * i : 4 * i + 4, 0:256] = piece
        tfeat[t] = jnp.transpose(fa[:, 0:256]).astype(jnp.bfloat16)
        return carry

    fa[40:PARTS, :] = jnp.zeros((PARTS - 40, 1024), jnp.float32)
    fb[40:PARTS, :] = jnp.zeros((PARTS - 40, 1024), jnp.float32)
    lax.fori_loop(0, 32, target_step, 0)

    for k in range(3):
        arrive(rt.at[k], p0r.at[k])
    total = wt[0] + rt[0] + rt[1] + rt[2]
    tile = jnp.where(c == 0, total[:, 0:128], total[:, 128:256])
    tail = jnp.where(c == 0, total[0:4, 256:384], total[4:8, 256:384])
    pv_ref[c, b, a, z, 0] = tile[0:4]
    pv_ref[c, b, a, z, 1] = tile[4:8]
    pv_ref[c, b, a, z, 2] = tail
    for k in (4, 3, 5, 2, 6, 1, 7):
        spot = pv_ref.at[c, b, a, z]
        send(spot, spot, zs.at[k - 1], zr.at[k - 1], ((z + k) % 8, gy))

    def prepare(t, feat, charge):
        for n in range(4):
            leaf = near_ref[n, t]
            v = win[jnp.clip(leaf - 32 * d + 32, 0, 95)]
            gap = jnp.where(spot_row == 0, leaf % 32 - t, 0)
            gap = jnp.where(spot_row == 1, (leaf // 32) % 32 - d % 32, gap)
            gap = jnp.where(spot_row == 2, leaf // 1024 - d // 32, gap)
            placed = jnp.where(spot_row < 3, v + 2.0 * gap.astype(jnp.float32), SOFT**0.5)
            for i, piece in enumerate(source_rows(placed)):
                feat[4 * i : 4 * i + 4, 256 * n : 256 * n + 256] = piece
            charge[0:1, 256 * n : 256 * n + 256] = v[3:4]

    def weigh(points, others, weights):
        count = others.shape[1]
        sums = []
        for i in range(0, 256, 64):
            pulled = lax.rsqrt(dot_n(points[i : i + 64], others)) * weights
            acc = pulled[:, 0:128]
            for j in range(128, count, 128):
                acc = acc + pulled[:, j : j + 128]
            sums.append(acc)
        return jnp.sum(jnp.transpose(jnp.concatenate(sums, axis=0)), axis=0, keepdims=True)

    def near_leaf(t, feat, charge):
        near_rows[pl.ds(t, 1), :] = weigh(tfeat[t], feat[...].astype(jnp.bfloat16), charge[0:1, :])

    def near_pair(i, carry):
        t = 2 * i
        prepare(t + 1, fb, qb)
        near_leaf(t, fa, qa)
        prepare(jnp.minimum(t + 2, 31), fa, qa)
        near_leaf(t + 1, fb, qb)
        return carry

    def near_part(k):
        if NEAR_SPLIT[k] < NEAR_SPLIT[k + 1]:
            lax.fori_loop(NEAR_SPLIT[k] // 2, NEAR_SPLIT[k + 1] // 2, near_pair, 0)

    for k in range(2):
        arrive(win.at[pl.ds(64 * k, 32)], hr.at[k])
    prepare(0, fa, qa)
    near_part(0)

    for k in (1, 7, 2, 6, 3, 5, 4):
        arrive(pv_ref.at[c, b, a, (z + 8 - k) % 8], zr.at[k - 1])
    forwards = 0

    def forward(spot):
        nonlocal forwards
        send(spot, spot, fs.at[forwards], fr.at[forwards], partner)
        forwards += 1

    spot = pv_ref.at[c, b, a]
    for k in (2, 1, 3):
        send(spot, spot, as_.at[k - 1], ar.at[k - 1], ab_dev((a + k) % 4, b))
    for k in (2, 1, 3):
        send(spot, spot, bs.at[0, k - 1], br.at[0, k - 1], ab_dev(a, (b + k) % 4))
    forward(spot)

    near_part(1)

    for j in (1, 3, 2):
        spot = pv_ref.at[c, b, (a + 4 - j) % 4]
        arrive(spot, ar.at[j - 1])
        for k in (2, 1, 3):
            send(spot, spot, bs.at[j, k - 1], br.at[j, k - 1], ab_dev(a, (b + k) % 4))
        forward(spot)

    for load in loads[4:]:
        load.wait()

    def split_step(i, carry):
        th[i], tl[i] = halves(trans[i])
        return carry

    lax.fori_loop(0, 16, split_step, 0)
    near_part(2)

    for k in range(2):
        arrive(dw.at[pl.ds(64 * k, 32)], hr.at[2 + k])

    def columns(ref):
        return jnp.transpose(ref[...])

    def choose(cols, count, width):
        lane = lax.broadcasted_iota(jnp.int32, (32, width), 1)
        return jnp.concatenate(
            [(cols[:, k : k + 1] == lane).astype(jnp.float32) for k in range(count)], axis=0
        ).astype(jnp.bfloat16)

    def by_class(ref, count):
        table = ref[...]
        pad = jnp.zeros((count, 96), jnp.int32)
        wide = jnp.concatenate([table, pad], axis=1)
        tiles = []
        for k in range(0, count, 4):
            row = wide[k : k + 1]
            for m in range(1, 4):
                row = row + pltpu.roll(wide[k + m : k + m + 1], 32 * m, 1)
            tiles.append(row)
        row = jnp.concatenate(tiles, axis=1)
        shape = (512, 32 * count)
        line = lax.broadcasted_iota(jnp.int32, shape, 0)
        lane = lax.broadcasted_iota(jnp.int32, shape, 1)
        code = row * 32 + lax.broadcasted_iota(jnp.int32, row.shape, 1) % 32
        return jnp.where(code == line, 1.0, 0.0).astype(jnp.bfloat16)

    far_pick = choose(columns(flist) - 32 * d + 32, 16, 96)
    dens_high, dens_low = halves(dw[...])
    far_high = dot_n(far_pick, dens_high).astype(jnp.bfloat16)
    far_low = dot_n(far_pick, dens_low).astype(jnp.bfloat16)
    far_class = by_class(fclass, 16)
    gfar[...] = dot_n(far_class, far_high) + dot_n(far_class, far_low)

    near_part(3)

    for j in (0, 1, 3, 2):
        for k in (1, 3, 2):
            spot = pv_ref.at[c, (b + 4 - k) % 4, (a + 4 - j) % 4]
            arrive(spot, br.at[j, k - 1])
            forward(spot)

    coarse_pick = choose(columns(clist), 8, 1024)
    coarse_class = by_class(cclass, 8)
    down_high, down_low = halves(down[...])

    n = 0
    arrive(pv_ref.at[1 - c, a, b], fr.at[n])
    n += 1
    for j in (1, 3, 2):
        arrive(pv_ref.at[1 - c, a, (b + 4 - j) % 4], fr.at[n])
        n += 1
    for j in (0, 1, 3, 2):
        for k in (1, 3, 2):
            arrive(pv_ref.at[1 - c, (a + 4 - k) % 4, (b + 4 - j) % 4], fr.at[n])
            n += 1

    def collect(i, carry):
        zz, xx, yy = i // 8, (i // 2) % 4, (i % 2) * 2
        parts = []
        for q in range(2):
            one, two_ = pv_ref[0, yy + q, xx, zz], pv_ref[1, xx, yy + q, zz]
            parts.append(
                jnp.concatenate(
                    [
                        jnp.concatenate([one[0], one[1]], axis=0),
                        jnp.concatenate([two_[0], two_[1]], axis=0),
                        jnp.concatenate([one[2], two_[2]], axis=0),
                    ],
                    axis=1,
                )
            )
        high, low = halves(jnp.concatenate(parts, axis=0))
        up_high[pl.ds(pl.multiple_of(16 * i, 16), 16), :] = high
        up_low[pl.ds(pl.multiple_of(16 * i, 16), 16), :] = low
        return carry

    lax.fori_loop(0, 64, collect, 0, unroll=8)
    coarse_high = dot_n(coarse_pick, up_high[...]).astype(jnp.bfloat16)
    coarse_low = dot_n(coarse_pick, up_low[...]).astype(jnp.bfloat16)
    gathered = gfar[...] + (dot_n(coarse_class, coarse_high) + dot_n(coarse_class, coarse_low))[:, 0:P_SIZE]
    g_high, g_low = halves(gathered)
    wide_sum = jnp.zeros((P_SIZE, 64), jnp.float32)
    slim_sum = jnp.zeros((P_SIZE, 32), jnp.float32)
    for i in range(16):
        high, low = g_high[32 * i : 32 * i + 32], g_low[32 * i : 32 * i + 32]
        wide_sum = wide_sum + dot_t(th[i], jnp.concatenate([high, low], axis=0))
        slim_sum = slim_sum + dot_t(tl[i], high)
    check = wide_sum[:, 0:32] + wide_sum[:, 32:64] + slim_sum
    c_high, c_low = halves(jnp.transpose(check))
    equiv[...] = jnp.zeros_like(equiv)
    equiv[:, 0:P_SIZE] = dot_t(c_high, down_high) + dot_t(c_low, down_high) + dot_t(c_high, down_low)

    out_lane = lax.broadcasted_iota(jnp.int32, (1, 256), 1)
    far_points = surf[...]

    def far_leaf(t, carry):
        row = near_rows[pl.ds(t, 1), :] + weigh(tfeat[t], far_points, equiv[pl.ds(t, 1), :])
        out_ref[pl.ds(t, 1), :] = jnp.where(out_lane < live_ref[t], row, 0.0)
        return carry

    lax.fori_loop(0, 32, far_leaf, 0, unroll=2)
    for cp in sends:
        cp.wait_send()


def surface_features():
    points = np.zeros((4, 384), np.float32)
    points[:3, :P_SIZE] = surface_rows()
    points[3, :] = SOFT**0.5
    points[:3, P_SIZE:] = HALF

    def short(v):
        return v.astype(jnp.bfloat16).astype(np.float32)

    high = short(points)
    low = short(points - high)
    seen = high + low
    square = seen * seen
    s1 = short(square)
    s2 = short(square - s1)
    s3 = short(square - s1 - s2)
    one = np.ones_like(points)
    rows = [-2 * high, -2 * low, -2 * high, -2 * low, s1, s2, s3, one, one, one]
    stacked = np.concatenate(rows + [np.zeros((PARTS - 40, 384), np.float32)], axis=0)
    return stacked.astype(jnp.bfloat16)


def on_device(
    sources, live_counts, densities, near_list, far_list, far_class, coarse_list, coarse_class, translations,
    check_to_equiv, up_check_to_equiv, partial_check, contrib_ids,
):
    smem = pl.BlockSpec(memory_space=pltpu.SMEM)
    hbm = pl.BlockSpec(memory_space=pl.ANY)
    vmem = pl.BlockSpec(memory_space=pltpu.VMEM)
    dma = pltpu.SemaphoreType.DMA
    f32, bf16, i32 = jnp.float32, jnp.bfloat16, jnp.int32
    return pl.pallas_call(
        fmm_kernel,
        out_shape=jax.ShapeDtypeStruct((32, 256), f32),
        in_specs=[smem, smem] + [hbm] * 12,
        out_specs=vmem,
        scratch_shapes=[
            pltpu.VMEM((2, 4, 4, 8, 3, 4, 128), f32),
            pltpu.VMEM((2, 8, 384), f32),
            pltpu.VMEM((3, 8, 384), f32),
            pltpu.VMEM((96, 4, 256), f32),
            pltpu.VMEM((96, P_SIZE), f32),
            pltpu.VMEM((16, 32), i32),
            pltpu.VMEM((16, 32), i32),
            pltpu.VMEM((8, 32), i32),
            pltpu.VMEM((8, 32), i32),
            pltpu.VMEM((16, P_SIZE, P_SIZE), f32),
            pltpu.VMEM((P_SIZE, P_SIZE), f32),
            pltpu.VMEM((P_SIZE, P_SIZE), f32),
            pltpu.VMEM((64, P_SIZE), f32),
            pltpu.VMEM((1, 64), i32),
            pltpu.VMEM((PARTS, 384), bf16),
            pltpu.VMEM((32, 256, PARTS), bf16),
            pltpu.VMEM((PARTS, 1024), f32),
            pltpu.VMEM((PARTS, 1024), f32),
            pltpu.VMEM((8, 1024), f32),
            pltpu.VMEM((8, 1024), f32),
            pltpu.VMEM((16, P_SIZE, P_SIZE), bf16),
            pltpu.VMEM((16, P_SIZE, P_SIZE), bf16),
            pltpu.VMEM((512, P_SIZE), f32),
            pltpu.VMEM((1024, 384), bf16),
            pltpu.VMEM((1024, 384), bf16),
            pltpu.VMEM((32, 384), f32),
            pltpu.VMEM((32, 256), f32),
            dma((3,)), dma((3,)), dma((4,)), dma((4,)), dma((7,)), dma((7,)),
            dma((3,)), dma((3,)), dma((4, 3)), dma((4, 3)), dma((16,)), dma((16,)), dma((12,)),
        ],
        compiler_params=pltpu.CompilerParams(
            collective_id=0, has_side_effects=True, vmem_limit_bytes=60 * 1024 * 1024
        ),
    )(
        near_list.T, live_counts, sources, densities.T, far_list.T, far_class.T, coarse_list.T, coarse_class.T,
        translations, check_to_equiv, up_check_to_equiv, partial_check[0].T, contrib_ids,
        jnp.asarray(surface_features()),
    )


def solution(mesh):
    both = ("gx", "gy")
    return jax.shard_map(
        on_device,
        mesh=mesh,
        in_specs=(
            P(both, None, None), P(both), P(None, both), P(both, None), P(both, None), P(both, None), P(both, None),
            P(both, None), P(), P(), P(), P(both, None, None), P(both, None),
        ),
        out_specs=P(both, None),
        check_vma=False,
    )
```

time: 85.1 us -> 46.9 us (0.55)
  other arithmetic: 27.4 us -> 0 us
  Pallas kernels: 35 us -> 45.2 us
  matrix products: 10.2 us -> 0 us
  local copies, waits for them, and re-layouts: 11.4 us -> 1.38 us
    reduce_sum x6 -> x0, other arithmetic: 22.8 us -> none  [the longest x4 18 us: near_block(): return jnp.sum(kernel * neighbours[:, :, 3, None, :], axis=(1, 3))]
    pallas_call x1, Pallas kernels: 35 us -> 45.2 us  [on_device(): pl.pallas_call(fmm_kernel, out_shape=jax.ShapeDtypeStruct((32, 256), f32)...]
    dot_general x4 -> x0, matrix products: 10.2 us -> none  [the longest x1 8.4 us: on_device(): jnp.einsum('cpq,cqt->pt', translations, gathered, precision=highest)]
    gather x6 -> x0, local copies, waits for them, and re-layouts: 5.11 us -> none  [the longest x4 2.53 us: near_step(): return near_block(targets, window[chosen])]
    select_n x10 -> x0, other arithmetic: 2.45 us -> none  [the longest x1 1.01 us: on_device(): charges = jnp.where(is_live, sources[:, 3, :], 0.0)]
    squeeze x11 -> x0, local copies, waits for them, and re-layouts: 2.34 us -> none  [the longest x1 1.35 us: on_device(): first = pieces[0]]
    transpose x3 -> x0, local copies, waits for them, and re-layouts: 1.51 us -> none  [the longest x1 1.22 us: on_device(): second = pieces[1].transpose(1, 0, 2, 3, 4, 5)]
    add x1 -> x0, other arithmetic: 1.01 us -> none  [on_device(): positions = sources[:, :3, :] + centres[:, :, None]]
where the time goes in v2:
time: 46.9 us; the launch traced here: 46.6 us
  Pallas kernels  45.2 us (96%)
  local copies, waits for them, and re-layouts  1.38 us (3%)
    pallas_call x1, Pallas kernels, on_device(): pl.pallas_call(fmm_kernel, out_shape=jax.ShapeDtypeStruct((32, 256), f32)...  45.2 us
    unnamed x1, local copies, waits for them, and re-layouts  1.38 us

profile of v2, /device:TPU:1, one launch (start us, length us, event | category | flops | bytes accessed | tf_op | source)
XLA Modules:
  0.0 46.6 jit_solution(18169924498026327128)
XLA Ops:
  0.0 45.2 %shard_map.136 = f32[32,256]{1,0:T(8,128)} custom-call(s32[4,32]{1,0:T(4,128)} %bitcast.15, s32[32]{0:T(128)} %live_ref.1, f32[32,4,256]{2,1,0:T(4,128)} %src_hbm.1, f32[32,296]{1,0:T(8,128)} %bitcast.10, s32[16,32]{1,0:T(8,128)} %bitcast.11, s32[16,32]{1,0:T(8,128)} %bitcast.12, s32[8,32]{1,0:T(8,128)} %bitcast.13, s32[8,32]{1,0:T(8,128)} %bitcast.14, ...), custom_call_target="tpu_custom_call" | custom-call | tf_op jit(solution)/shard_map/pallas_call | solution.py:403
  45.2 1.4 %copy.16 = f32[32,256]{1,0:T(8,128)} copy(f32[32,256]{1,0:T(8,128)} %shard_map.136) | data formatting | bytes 65536

commit v3 on v2

--- a/solution.py
+++ b/solution.py
@@ -12,7 +12,7 @@
 SOFT = 0.0625
 HALF = 2.5
 PARTS = 48
-NEAR_SPLIT = (0, 8, 14, 32, 32)
+NEAR_SPLIT = (0, 8, 16, 20, 24, 28, 32)
 
 
 def surface_rows():
@@ -64,7 +64,7 @@
     near_ref, live_ref, src_hbm, dens_hbm, flist_hbm, fclass_hbm, clist_hbm, cclass_hbm, trans_hbm, down_hbm, up_hbm,
     part_hbm, ids_hbm, surf_hbm, out_ref,
     pv_ref, wt, rt, win, dw, flist, fclass, clist, cclass, trans, down, up, part, ids, surf,
-    tfeat, fa, fb, qa, qb, th, tl, gfar, up_high, up_low, equiv, near_rows,
+    tfeat, tfar, fa, fb, qa, qb, th, tl, gfar, up_high, up_low, pulls, near_rows,
     p0s, p0r, hs, hr, zs, zr, as_, ar, bs, br, fs, fr, ls,
 ):
     highest = lax.Precision.HIGHEST
@@ -165,11 +165,20 @@
         for i, piece in enumerate(target_rows(v)):
             fa[4 * i : 4 * i + 4, 0:256] = piece
         tfeat[t] = jnp.transpose(fa[:, 0:256]).astype(jnp.bfloat16)
+        tfar[t] = fa[:, 0:256].astype(jnp.bfloat16)
         return carry
 
     fa[40:PARTS, :] = jnp.zeros((PARTS - 40, 1024), jnp.float32)
     fb[40:PARTS, :] = jnp.zeros((PARTS - 40, 1024), jnp.float32)
-    lax.fori_loop(0, 32, target_step, 0)
+    lax.fori_loop(0, 32, target_step, 0, unroll=4)
+    loads[9].wait()
+    far_points = surf
+
+    def pull_step(t, carry):
+        pulls[t] = lax.rsqrt(dot_n(far_points[...], tfar[t]))
+        return carry
+
+    lax.fori_loop(0, 32, pull_step, 0, unroll=8)
 
     for k in range(3):
         arrive(rt.at[k], p0r.at[k])
@@ -219,8 +228,27 @@
 
     def near_part(k):
         if NEAR_SPLIT[k] < NEAR_SPLIT[k + 1]:
-            lax.fori_loop(NEAR_SPLIT[k] // 2, NEAR_SPLIT[k + 1] // 2, near_pair, 0)
-
+            lax.fori_loop(NEAR_SPLIT[k] // 2, NEAR_SPLIT[k + 1] // 2, near_pair, 0, unroll=2)
+
+    for load in loads[4:9] + loads[10:]:
+        load.wait()
+
+    def split_step(i, carry):
+        v = trans[i]
+        at = pl.ds(pl.multiple_of(256 * i, 256), 256)
+        th[:, at], tl[:, at] = halves(v[:, 0:256])
+        return carry
+
+    lax.fori_loop(0, 16, split_step, 0, unroll=2)
+    lane = lax.broadcasted_iota(jnp.int32, (P_SIZE, 128), 1)
+    blank = jnp.zeros((P_SIZE, 88), jnp.float32)
+    for i in range(0, 16, 3):
+        packed = jnp.zeros((P_SIZE, 128), jnp.float32)
+        for m in range(min(3, 16 - i)):
+            piece = jnp.concatenate([trans[i + m, :, 256:P_SIZE], blank], axis=1)
+            packed = packed + (pltpu.roll(piece, 40 * m, 1) if m else piece)
+        at = 4096 + 128 * (i // 3)
+        th[:, at : at + 128], tl[:, at : at + 128] = halves(packed)
     for k in range(2):
         arrive(win.at[pl.ds(64 * k, 32)], hr.at[k])
     prepare(0, fa, qa)
@@ -238,7 +266,7 @@
     spot = pv_ref.at[c, b, a]
     for k in (2, 1, 3):
         send(spot, spot, as_.at[k - 1], ar.at[k - 1], ab_dev((a + k) % 4, b))
-    for k in (2, 1, 3):
+    for k in (1, 3):
         send(spot, spot, bs.at[0, k - 1], br.at[0, k - 1], ab_dev(a, (b + k) % 4))
     forward(spot)
 
@@ -247,20 +275,26 @@
     for j in (1, 3, 2):
         spot = pv_ref.at[c, b, (a + 4 - j) % 4]
         arrive(spot, ar.at[j - 1])
-        for k in (2, 1, 3):
+        for k in (1, 3):
             send(spot, spot, bs.at[j, k - 1], br.at[j, k - 1], ab_dev(a, (b + k) % 4))
         forward(spot)
 
-    for load in loads[4:]:
-        load.wait()
-
-    def split_step(i, carry):
-        th[i], tl[i] = halves(trans[i])
-        return carry
-
-    lax.fori_loop(0, 16, split_step, 0)
+    def b_step(j):
+        for k in (1, 3):
+            spot = pv_ref.at[c, (b + 4 - k) % 4, (a + 4 - j) % 4]
+            arrive(spot, br.at[j, k - 1])
+            if (j in (0, 3)) == (k == 1):
+                send(spot, spot, bs.at[j, 1], br.at[j, 1], ab_dev(a, (b + k) % 4))
+            forward(spot)
+
     near_part(2)
-
+    b_step(0)
+    near_part(3)
+    b_step(1)
+    near_part(4)
+    b_step(3)
+    near_part(5)
+    b_step(2)
     for k in range(2):
         arrive(dw.at[pl.ds(64 * k, 32)], hr.at[2 + k])
 
@@ -295,19 +329,17 @@
     far_high = dot_n(far_pick, dens_high).astype(jnp.bfloat16)
     far_low = dot_n(far_pick, dens_low).astype(jnp.bfloat16)
     far_class = by_class(fclass, 16)
-    gfar[...] = dot_n(far_class, far_high) + dot_n(far_class, far_low)
-
-    near_part(3)
-
-    for j in (0, 1, 3, 2):
-        for k in (1, 3, 2):
-            spot = pv_ref.at[c, (b + 4 - k) % 4, (a + 4 - j) % 4]
-            arrive(spot, br.at[j, k - 1])
-            forward(spot)
+    gfar[...] = jnp.zeros_like(gfar)
+    gfar[:, 0:P_SIZE] = dot_n(far_class, far_high) + dot_n(far_class, far_low)
 
     coarse_pick = choose(columns(clist), 8, 1024)
     coarse_class = by_class(cclass, 8)
     down_high, down_low = halves(down[...])
+
+    for j in (0, 1, 3, 2):
+        spot = pv_ref.at[c, (b + 2) % 4, (a + 4 - j) % 4]
+        arrive(spot, br.at[j, 1])
+        forward(spot)
 
     n = 0
     arrive(pv_ref.at[1 - c, a, b], fr.at[n])
@@ -316,9 +348,12 @@
         arrive(pv_ref.at[1 - c, a, (b + 4 - j) % 4], fr.at[n])
         n += 1
     for j in (0, 1, 3, 2):
-        for k in (1, 3, 2):
+        for k in (1, 3):
             arrive(pv_ref.at[1 - c, (a + 4 - k) % 4, (b + 4 - j) % 4], fr.at[n])
             n += 1
+    for j in (0, 1, 3, 2):
+        arrive(pv_ref.at[1 - c, (a + 2) % 4, (b + 4 - j) % 4], fr.at[n])
+        n += 1
 
     def collect(i, carry):
         zz, xx, yy = i // 8, (i // 2) % 4, (i % 2) * 2
@@ -343,37 +378,28 @@
     lax.fori_loop(0, 64, collect, 0, unroll=8)
     coarse_high = dot_n(coarse_pick, up_high[...]).astype(jnp.bfloat16)
     coarse_low = dot_n(coarse_pick, up_low[...]).astype(jnp.bfloat16)
-    gathered = gfar[...] + (dot_n(coarse_class, coarse_high) + dot_n(coarse_class, coarse_low))[:, 0:P_SIZE]
-    g_high, g_low = halves(gathered)
-    wide_sum = jnp.zeros((P_SIZE, 64), jnp.float32)
-    slim_sum = jnp.zeros((P_SIZE, 32), jnp.float32)
-    for i in range(16):
-        high, low = g_high[32 * i : 32 * i + 32], g_low[32 * i : 32 * i + 32]
-        wide_sum = wide_sum + dot_t(th[i], jnp.concatenate([high, low], axis=0))
-        slim_sum = slim_sum + dot_t(tl[i], high)
-    check = wide_sum[:, 0:32] + wide_sum[:, 32:64] + slim_sum
-    c_high, c_low = halves(jnp.transpose(check))
-    equiv[...] = jnp.zeros_like(equiv)
-    equiv[:, 0:P_SIZE] = dot_t(c_high, down_high) + dot_t(c_low, down_high) + dot_t(c_high, down_low)
-
-    out_lane = lax.broadcasted_iota(jnp.int32, (1, 256), 1)
-    far_points = surf[...]
-
-    def far_leaf(t, carry):
-        row = near_rows[pl.ds(t, 1), :] + weigh(tfeat[t], far_points, equiv[pl.ds(t, 1), :])
-        out_ref[pl.ds(t, 1), :] = jnp.where(out_lane < live_ref[t], row, 0.0)
-        return carry
-
-    lax.fori_loop(0, 32, far_leaf, 0, unroll=2)
+    gathered = gfar[...] + dot_n(coarse_class, coarse_high) + dot_n(coarse_class, coarse_low)
+    ends = []
+    for i in range(0, 16, 3):
+        packed = gathered[32 * i : 32 * i + 32, 256:384]
+        for m in range(1, min(3, 16 - i)):
+            packed = packed + pltpu.roll(gathered[32 * (i + m) : 32 * (i + m) + 32, 256:384], 40 * m, 1)
+        ends.append(packed)
+    spread = jnp.concatenate([gathered[32 * i : 32 * i + 32, 0:256] for i in range(16)] + ends, axis=1)
+    g_high, g_low = halves(spread)
+    wide_sum = dot_t(th[...], jnp.concatenate([g_high, g_low], axis=0))
+    check = wide_sum[:, 0:32] + wide_sum[:, 32:64] + dot_t(tl[...], g_high)
+    c_high, c_low = halves(check)
+    equiv = dot_n(down_high, c_high) + dot_n(down_high, c_low) + dot_n(down_low, c_high)
+    for t in range(32):
+        far = jnp.sum(equiv[:, t : t + 1] * pulls[t], axis=0, keepdims=True)
+        out_ref[t : t + 1, :] = near_rows[t : t + 1, :] + far
     for cp in sends:
         cp.wait_send()
 
 
 def surface_features():
-    points = np.zeros((4, 384), np.float32)
-    points[:3, :P_SIZE] = surface_rows()
-    points[3, :] = SOFT**0.5
-    points[:3, P_SIZE:] = HALF
+    points = np.concatenate([surface_rows(), np.full((1, P_SIZE), SOFT**0.5, np.float32)], axis=0)
 
     def short(v):
         return v.astype(jnp.bfloat16).astype(np.float32)
@@ -387,8 +413,8 @@
     s3 = short(square - s1 - s2)
     one = np.ones_like(points)
     rows = [-2 * high, -2 * low, -2 * high, -2 * low, s1, s2, s3, one, one, one]
-    stacked = np.concatenate(rows + [np.zeros((PARTS - 40, 384), np.float32)], axis=0)
-    return stacked.astype(jnp.bfloat16)
+    stacked = np.concatenate(rows + [np.zeros((PARTS - 40, P_SIZE), np.float32)], axis=0)
+    return np.ascontiguousarray(stacked.T).astype(jnp.bfloat16)
 
 
 def on_device(
@@ -400,7 +426,7 @@
     vmem = pl.BlockSpec(memory_space=pltpu.VMEM)
     dma = pltpu.SemaphoreType.DMA
     f32, bf16, i32 = jnp.float32, jnp.bfloat16, jnp.int32
-    return pl.pallas_call(
+    sums = pl.pallas_call(
         fmm_kernel,
         out_shape=jax.ShapeDtypeStruct((32, 256), f32),
         in_specs=[smem, smem] + [hbm] * 12,
@@ -420,18 +446,19 @@
             pltpu.VMEM((P_SIZE, P_SIZE), f32),
             pltpu.VMEM((64, P_SIZE), f32),
             pltpu.VMEM((1, 64), i32),
-            pltpu.VMEM((PARTS, 384), bf16),
+            pltpu.VMEM((P_SIZE, PARTS), bf16),
             pltpu.VMEM((32, 256, PARTS), bf16),
+            pltpu.VMEM((32, PARTS, 256), bf16),
             pltpu.VMEM((PARTS, 1024), f32),
             pltpu.VMEM((PARTS, 1024), f32),
             pltpu.VMEM((8, 1024), f32),
             pltpu.VMEM((8, 1024), f32),
-            pltpu.VMEM((16, P_SIZE, P_SIZE), bf16),
-            pltpu.VMEM((16, P_SIZE, P_SIZE), bf16),
-            pltpu.VMEM((512, P_SIZE), f32),
+            pltpu.VMEM((P_SIZE, 4864), bf16),
+            pltpu.VMEM((P_SIZE, 4864), bf16),
+            pltpu.VMEM((512, 384), f32),
             pltpu.VMEM((1024, 384), bf16),
             pltpu.VMEM((1024, 384), bf16),
-            pltpu.VMEM((32, 384), f32),
+            pltpu.VMEM((32, P_SIZE, 256), f32),
             pltpu.VMEM((32, 256), f32),
             dma((3,)), dma((3,)), dma((4,)), dma((4,)), dma((7,)), dma((7,)),
             dma((3,)), dma((3,)), dma((4, 3)), dma((4, 3)), dma((16,)), dma((16,)), dma((12,)),
@@ -444,6 +471,7 @@
         translations, check_to_equiv, up_check_to_equiv, partial_check[0].T, contrib_ids,
         jnp.asarray(surface_features()),
     )
+    return jnp.where(jnp.arange(256, dtype=jnp.int32)[None, :] < live_counts[:, None], sums, 0.0)
 
 
 def solution(mesh):

time: 46.9 us -> 42.9 us (0.915)
  Pallas kernels: 45.2 us -> 41.3 us
  other arithmetic: 0 us -> 1.45 us
  local copies, waits for them, and re-layouts: 1.38 us -> 0.01 us
    pallas_call x1, Pallas kernels: 45.2 us -> 41.3 us  [on_device(): pl.pallas_call(fmm_kernel, out_shape=jax.ShapeDtypeStruct((32, 256), f32)...]
    select_n x0 -> x1, other arithmetic: none -> 1.45 us  [on_device(): jnp.where(jnp.arange(256, dtype=jnp.int32)[None, :] < live_counts[:, None...]
    unnamed x1 -> x2, local copies, waits for them, and re-layouts: 1.38 us -> 0.01 us
where the time goes in v3:
time: 42.9 us; the launch traced here: 42.7 us
  Pallas kernels  41.3 us (96%)
  other arithmetic  1.45 us (3%)
    pallas_call x1, Pallas kernels, on_device(): pl.pallas_call(fmm_kernel, out_shape=jax.ShapeDtypeStruct((32, 256), f32)...  41.3 us
    select_n x1, other arithmetic, on_device(): jnp.where(jnp.arange(256, dtype=jnp.int32)[None, :] < live_counts[:, None...  1.45 us

profile of v3, /device:TPU:1, one launch (start us, length us, event | category | flops | bytes accessed | tf_op | source)
XLA Modules:
  0.0 42.7 jit_solution(1334442774627066933)
XLA Ops:
  0.0 0.0 copy-start
  0.0 41.3 %shard_map.136 = f32[32,256]{1,0:T(8,128)} custom-call(s32[4,32]{1,0:T(4,128)} %bitcast.15, s32[32]{0:T(128)} %live_ref.1, f32[32,4,256]{2,1,0:T(4,128)} %src_hbm.1, f32[32,296]{1,0:T(8,128)} %bitcast.10, s32[16,32]{1,0:T(8,128)} %bitcast.11, s32[16,32]{1,0:T(8,128)} %bitcast.12, s32[8,32]{1,0:T(8,128)} %bitcast.13, s32[8,32]{1,0:T(8,128)} %bitcast.14, ...), custom_call_target="tpu_custom_call" | custom-call | tf_op jit(solution)/shard_map/pallas_call | solution.py:429
  41.3 0.0 copy-done
  41.3 1.4 %fusion = f32[32,256]{1,0:T(8,128)} fusion(f32[32,256]{1,0:T(8,128)} %shard_map.136, s32[32]{0:T(128)S(1)} %copy-done), kind=kLoop, calls=%fused_computation.1 | loop fusion | flops 16384 | bytes 65664 | tf_op jit(solution)/shard_map/jit(_where)/select_n | solution.py:474
Async XLA Ops:
  0.0 41.3 %copy-start = (s32[32]{0:T(128)S(1)}, s32[32]{0:T(128)}, u32[]{:S(2)}) copy-start(s32[32]{0:T(128)} %live_ref.1) | copy-start | bytes 388

commit v4 on v3

--- a/solution.py
+++ b/solution.py
@@ -61,11 +61,11 @@
 
 
 def fmm_kernel(
-    near_ref, live_ref, src_hbm, dens_hbm, flist_hbm, fclass_hbm, clist_hbm, cclass_hbm, trans_hbm, down_hbm, up_hbm,
+    near_hbm, live_hbm, src_hbm, dens_hbm, flist_hbm, fclass_hbm, clist_hbm, cclass_hbm, trans_hbm, down_hbm, up_hbm,
     part_hbm, ids_hbm, surf_hbm, out_ref,
     pv_ref, wt, rt, win, dw, flist, fclass, clist, cclass, trans, down, up, part, ids, surf,
     tfeat, tfar, fa, fb, qa, qb, th, tl, gfar, up_high, up_low, pulls, near_rows,
-    p0s, p0r, hs, hr, zs, zr, as_, ar, bs, br, fs, fr, ls,
+    near_ref, live_ref, p0s, p0r, hs, hr, zs, zr, as_, ar, bs, br, fs, fr, ls,
 ):
     highest = lax.Precision.HIGHEST
     z = lax.axis_index("gx")
@@ -102,6 +102,7 @@
                 (ids_hbm, ids), (part_hbm, part), (up_hbm, up), (src_hbm, win.at[pl.ds(32, 32)]),
                 (dens_hbm, dw.at[pl.ds(32, 32)]), (flist_hbm, flist), (fclass_hbm, fclass), (clist_hbm, clist),
                 (cclass_hbm, cclass), (surf_hbm, surf), (down_hbm, down), (trans_hbm, trans),
+                (near_hbm, near_ref), (live_hbm, live_ref),
             )
         )
     ]
@@ -116,22 +117,11 @@
         load.wait()
     hot = (wanted == ids[...]).astype(jnp.float32)
     mine = jnp.dot(hot, part[...], precision=highest, preferred_element_type=jnp.float32)
-    mine = lax.dot_general(
-        mine, up[...], (((1,), (1,)), ((), ())), precision=highest, preferred_element_type=jnp.float32
-    )
+    m_high, m_low = halves(mine)
+    u_high, u_low = halves(up[...])
+    mine = dot_t(m_high, u_high) + dot_t(m_low, u_high) + dot_t(m_high, u_low)
     wt[0, :, 0:P_SIZE] = mine[0:8]
     wt[1, :, 0:P_SIZE] = mine[8:16]
-    loads[3].wait()
-    spot_row = lax.broadcasted_iota(jnp.int32, (4, 256), 0)
-    spot_lane = lax.broadcasted_iota(jnp.int32, (4, 256), 1)
-
-    def mask_leaf(t, carry):
-        v = win[32 + t]
-        win[32 + t] = jnp.where((spot_row == 3) & (spot_lane >= live_ref[t]), 0.0, v)
-        return carry
-
-    lax.fori_loop(0, 32, mask_leaf, 0)
-
     pl.semaphore_wait(barrier, len(peers))
 
     def rcopy(src, dst, ssem, rsem, dev):
@@ -152,6 +142,18 @@
     send(wt.at[1], rt.at[2 - c], p0s.at[1], p0r.at[2 - c], chip_dev(adj_chip, 0))
     send(wt.at[1], rt.at[2 - c], p0s.at[2], p0r.at[2 - c], chip_dev(adj_chip, 1))
     send(wt.at[0], rt.at[0], p0s.at[0], p0r.at[0], partner)
+    loads[3].wait()
+    loads[13].wait()
+    spot_row = lax.broadcasted_iota(jnp.int32, (4, 256), 0)
+    spot_lane = lax.broadcasted_iota(jnp.int32, (4, 256), 1)
+
+    def mask_leaf(t, carry):
+        v = win[32 + t]
+        win[32 + t] = jnp.where((spot_row == 3) & (spot_lane >= live_ref[t]), 0.0, v)
+        return carry
+
+    lax.fori_loop(0, 32, mask_leaf, 0, unroll=4)
+
     up_d, down_d = (d + 1) % 256, (d + 255) % 256
     up_dev, down_dev = (up_d // 32, up_d % 32), (down_d // 32, down_d % 32)
     own = win.at[pl.ds(32, 32)]
@@ -230,7 +232,7 @@
         if NEAR_SPLIT[k] < NEAR_SPLIT[k + 1]:
             lax.fori_loop(NEAR_SPLIT[k] // 2, NEAR_SPLIT[k + 1] // 2, near_pair, 0, unroll=2)
 
-    for load in loads[4:9] + loads[10:]:
+    for load in loads[4:9] + loads[10:13]:
         load.wait()
 
     def split_step(i, carry):
@@ -332,7 +334,9 @@
     gfar[...] = jnp.zeros_like(gfar)
     gfar[:, 0:P_SIZE] = dot_n(far_class, far_high) + dot_n(far_class, far_low)
 
-    coarse_pick = choose(columns(clist), 8, 1024)
+    wanted = clist[...]
+    spots = ((wanted // 8) % 16) * 64 + (wanted // 128) * 8 + wanted % 8
+    coarse_pick = choose(jnp.transpose(spots), 8, 1024)
     coarse_class = by_class(cclass, 8)
     down_high, down_low = halves(down[...])
 
@@ -341,9 +345,8 @@
         arrive(spot, br.at[j, 1])
         forward(spot)
 
-    n = 0
-    arrive(pv_ref.at[1 - c, a, b], fr.at[n])
-    n += 1
+    arrive(pv_ref.at[1 - c, a, b], fr.at[0])
+    n = 1
     for j in (1, 3, 2):
         arrive(pv_ref.at[1 - c, a, (b + 4 - j) % 4], fr.at[n])
         n += 1
@@ -351,31 +354,49 @@
         for k in (1, 3):
             arrive(pv_ref.at[1 - c, (a + 4 - k) % 4, (b + 4 - j) % 4], fr.at[n])
             n += 1
+
+    def collect(da, db):
+        a1, b1 = (a + da) % 4, (b + db) % 4
+        xx, yy = a1 + c * (b1 - a1), b1 + c * (a1 - b1)
+        base = (xx * 4 + yy) * 64
+        for k in range(4):
+            parts = []
+            for zz in (2 * k, 2 * k + 1):
+                one, two_ = pv_ref[0, yy, xx, zz], pv_ref[1, xx, yy, zz]
+                parts.append(
+                    jnp.concatenate(
+                        [
+                            jnp.concatenate([one[0], one[1]], axis=0),
+                            jnp.concatenate([two_[0], two_[1]], axis=0),
+                            jnp.concatenate([one[2], two_[2]], axis=0),
+                        ],
+                        axis=1,
+                    )
+                )
+            high, low = halves(jnp.concatenate(parts, axis=0))
+            at = pl.ds(pl.multiple_of(base + 16 * k, 16), 16)
+            up_high[at, :] = high
+            up_low[at, :] = low
+
+    def collect_near(i, carry):
+        p, q = i // 3, i % 3
+        collect(p + p // 2, q + q // 2)
+        return carry
+
+    def collect_far(i, carry):
+        collect(2, i)
+        return carry
+
+    def collect_side(i, carry):
+        collect(i + i // 2, 2)
+        return carry
+
+    lax.fori_loop(0, 9, collect_near, 0, unroll=3)
     for j in (0, 1, 3, 2):
         arrive(pv_ref.at[1 - c, (a + 2) % 4, (b + 4 - j) % 4], fr.at[n])
         n += 1
-
-    def collect(i, carry):
-        zz, xx, yy = i // 8, (i // 2) % 4, (i % 2) * 2
-        parts = []
-        for q in range(2):
-            one, two_ = pv_ref[0, yy + q, xx, zz], pv_ref[1, xx, yy + q, zz]
-            parts.append(
-                jnp.concatenate(
-                    [
-                        jnp.concatenate([one[0], one[1]], axis=0),
-                        jnp.concatenate([two_[0], two_[1]], axis=0),
-                        jnp.concatenate([one[2], two_[2]], axis=0),
-                    ],
-                    axis=1,
-                )
-            )
-        high, low = halves(jnp.concatenate(parts, axis=0))
-        up_high[pl.ds(pl.multiple_of(16 * i, 16), 16), :] = high
-        up_low[pl.ds(pl.multiple_of(16 * i, 16), 16), :] = low
-        return carry
-
-    lax.fori_loop(0, 64, collect, 0, unroll=8)
+    lax.fori_loop(0, 4, collect_far, 0, unroll=2)
+    lax.fori_loop(0, 3, collect_side, 0, unroll=3)
     coarse_high = dot_n(coarse_pick, up_high[...]).astype(jnp.bfloat16)
     coarse_low = dot_n(coarse_pick, up_low[...]).astype(jnp.bfloat16)
     gathered = gfar[...] + dot_n(coarse_class, coarse_high) + dot_n(coarse_class, coarse_low)
@@ -421,7 +442,6 @@
     sources, live_counts, densities, near_list, far_list, far_class, coarse_list, coarse_class, translations,
     check_to_equiv, up_check_to_equiv, partial_check, contrib_ids,
 ):
-    smem = pl.BlockSpec(memory_space=pltpu.SMEM)
     hbm = pl.BlockSpec(memory_space=pl.ANY)
     vmem = pl.BlockSpec(memory_space=pltpu.VMEM)
     dma = pltpu.SemaphoreType.DMA
@@ -429,7 +449,7 @@
     sums = pl.pallas_call(
         fmm_kernel,
         out_shape=jax.ShapeDtypeStruct((32, 256), f32),
-        in_specs=[smem, smem] + [hbm] * 12,
+        in_specs=[hbm] * 14,
         out_specs=vmem,
         scratch_shapes=[
             pltpu.VMEM((2, 4, 4, 8, 3, 4, 128), f32),
@@ -460,8 +480,10 @@
             pltpu.VMEM((1024, 384), bf16),
             pltpu.VMEM((32, P_SIZE, 256), f32),
             pltpu.VMEM((32, 256), f32),
+            pltpu.SMEM((4, 32), i32),
+            pltpu.SMEM((32,), i32),
             dma((3,)), dma((3,)), dma((4,)), dma((4,)), dma((7,)), dma((7,)),
-            dma((3,)), dma((3,)), dma((4, 3)), dma((4, 3)), dma((16,)), dma((16,)), dma((12,)),
+            dma((3,)), dma((3,)), dma((4, 3)), dma((4, 3)), dma((16,)), dma((16,)), dma((14,)),
         ],
         compiler_params=pltpu.CompilerParams(
             collective_id=0, has_side_effects=True, vmem_limit_bytes=60 * 1024 * 1024

time: 42.9 us -> 41 us (0.956)
  Pallas kernels: 41.3 us -> 39.4 us
    pallas_call x1, Pallas kernels: 41.3 us -> 39.4 us  [on_device(): pl.pallas_call(fmm_kernel, out_shape=jax.ShapeDtypeStruct((32, 256), f32)...]
where the time goes in v4:
time: 41 us; the launch traced here: 40.9 us
  Pallas kernels  39.4 us (96%)
  other arithmetic  1.45 us (4%)
    pallas_call x1, Pallas kernels, on_device(): pl.pallas_call(fmm_kernel, out_shape=jax.ShapeDtypeStruct((32, 256), f32)...  39.4 us
    select_n x1, other arithmetic, on_device(): jnp.where(jnp.arange(256, dtype=jnp.int32)[None, :] < live_counts[:, None...  1.45 us

profile of v4, /device:TPU:1, one launch (start us, length us, event | category | flops | bytes accessed | tf_op | source)
XLA Modules:
  0.0 40.9 jit_solution(4053131946906385661)
XLA Ops:
  0.0 0.0 copy-start
  0.0 39.4 %shard_map.136 = f32[32,256]{1,0:T(8,128)} custom-call(s32[4,32]{1,0:T(4,128)} %bitcast.15, s32[32]{0:T(128)} %live_hbm.1, f32[32,4,256]{2,1,0:T(4,128)} %src_hbm.1, f32[32,296]{1,0:T(8,128)} %bitcast.10, s32[16,32]{1,0:T(8,128)} %bitcast.11, s32[16,32]{1,0:T(8,128)} %bitcast.12, s32[8,32]{1,0:T(8,128)} %bitcast.13, s32[8,32]{1,0:T(8,128)} %bitcast.14, ...), custom_call_target="tpu_custom_call" | custom-call | tf_op jit(solution)/shard_map/pallas_call | solution.py:449
  39.4 0.0 copy-done
  39.4 1.4 %fusion = f32[32,256]{1,0:T(8,128)} fusion(f32[32,256]{1,0:T(8,128)} %shard_map.136, s32[32]{0:T(128)S(1)} %copy-done), kind=kLoop, calls=%fused_computation.1 | loop fusion | flops 16384 | bytes 65664 | tf_op jit(solution)/shard_map/jit(_where)/select_n | solution.py:496
Async XLA Ops:
  0.0 39.4 %copy-start = (s32[32]{0:T(128)S(1)}, s32[32]{0:T(128)}, u32[]{:S(2)}) copy-start(s32[32]{0:T(128)} %live_hbm.1) | copy-start | bytes 388

commit v5 on v4

--- a/solution.py
+++ b/solution.py
@@ -64,7 +64,7 @@
     near_hbm, live_hbm, src_hbm, dens_hbm, flist_hbm, fclass_hbm, clist_hbm, cclass_hbm, trans_hbm, down_hbm, up_hbm,
     part_hbm, ids_hbm, surf_hbm, out_ref,
     pv_ref, wt, rt, win, dw, flist, fclass, clist, cclass, trans, down, up, part, ids, surf,
-    tfeat, tfar, fa, fb, qa, qb, th, tl, gfar, up_high, up_low, pulls, near_rows,
+    tfeat, tfar, fa, fb, qa, qb, th, tl, gfar, up_both, pulls, near_rows,
     near_ref, live_ref, p0s, p0r, hs, hr, zs, zr, as_, ar, bs, br, fs, fr, ls,
 ):
     highest = lax.Precision.HIGHEST
@@ -290,13 +290,13 @@
             forward(spot)
 
     near_part(2)
+    near_part(3)
     b_step(0)
-    near_part(3)
+    near_part(4)
     b_step(1)
-    near_part(4)
     b_step(3)
+    b_step(2)
     near_part(5)
-    b_step(2)
     for k in range(2):
         arrive(dw.at[pl.ds(64 * k, 32)], hr.at[2 + k])
 
@@ -375,8 +375,8 @@
                 )
             high, low = halves(jnp.concatenate(parts, axis=0))
             at = pl.ds(pl.multiple_of(base + 16 * k, 16), 16)
-            up_high[at, :] = high
-            up_low[at, :] = low
+            up_both[at, 0:384] = high
+            up_both[at, 384:768] = low
 
     def collect_near(i, carry):
         p, q = i // 3, i % 3
@@ -397,9 +397,8 @@
         n += 1
     lax.fori_loop(0, 4, collect_far, 0, unroll=2)
     lax.fori_loop(0, 3, collect_side, 0, unroll=3)
-    coarse_high = dot_n(coarse_pick, up_high[...]).astype(jnp.bfloat16)
-    coarse_low = dot_n(coarse_pick, up_low[...]).astype(jnp.bfloat16)
-    gathered = gfar[...] + dot_n(coarse_class, coarse_high) + dot_n(coarse_class, coarse_low)
+    coarse = dot_n(coarse_class, dot_n(coarse_pick, up_both[...]).astype(jnp.bfloat16))
+    gathered = gfar[...] + coarse[:, 0:384] + coarse[:, 384:768]
     ends = []
     for i in range(0, 16, 3):
         packed = gathered[32 * i : 32 * i + 32, 256:384]
@@ -413,7 +412,12 @@
     c_high, c_low = halves(check)
     equiv = dot_n(down_high, c_high) + dot_n(down_high, c_low) + dot_n(down_low, c_high)
     for t in range(32):
-        far = jnp.sum(equiv[:, t : t + 1] * pulls[t], axis=0, keepdims=True)
+        acc = jnp.zeros((8, 256), jnp.float32)
+        for lo in range(0, P_SIZE, 64):
+            hi = min(lo + 64, P_SIZE)
+            part_sum = equiv[lo:hi, t : t + 1] * pulls[t, lo:hi, :]
+            acc = acc + jnp.sum(part_sum.reshape((hi - lo) // 8, 8, 256), axis=0)
+        far = jnp.sum(acc, axis=0, keepdims=True)
         out_ref[t : t + 1, :] = near_rows[t : t + 1, :] + far
     for cp in sends:
         cp.wait_send()
@@ -476,8 +480,7 @@
             pltpu.VMEM((P_SIZE, 4864), bf16),
             pltpu.VMEM((P_SIZE, 4864), bf16),
             pltpu.VMEM((512, 384), f32),
-            pltpu.VMEM((1024, 384), bf16),
-            pltpu.VMEM((1024, 384), bf16),
+            pltpu.VMEM((1024, 768), bf16),
             pltpu.VMEM((32, P_SIZE, 256), f32),
             pltpu.VMEM((32, 256), f32),
             pltpu.SMEM((4, 32), i32),
@@ -486,7 +489,7 @@
             dma((3,)), dma((3,)), dma((4, 3)), dma((4, 3)), dma((16,)), dma((16,)), dma((14,)),
         ],
         compiler_params=pltpu.CompilerParams(
-            collective_id=0, has_side_effects=True, vmem_limit_bytes=60 * 1024 * 1024
+            collective_id=0, has_side_effects=True, vmem_limit_bytes=57 * 1024 * 1024
         ),
     )(
         near_list.T, live_counts, sources, densities.T, far_list.T, far_class.T, coarse_list.T, coarse_class.T,

time: 41 us -> 41.3 us (level)
  no operation moved by 1% of the time
where the time goes in v5:
time: 41.3 us; the launch traced here: 41.1 us
  Pallas kernels  39.7 us (96%)
  other arithmetic  1.45 us (4%)
    pallas_call x1, Pallas kernels, on_device(): pl.pallas_call(fmm_kernel, out_shape=jax.ShapeDtypeStruct((32, 256), f32)...  39.7 us
    select_n x1, other arithmetic, on_device(): jnp.where(jnp.arange(256, dtype=jnp.int32)[None, :] < live_counts[:, None...  1.45 us

profile of v5, /device:TPU:1, one launch (start us, length us, event | category | flops | bytes accessed | tf_op | source)
XLA Modules:
  0.0 41.1 jit_solution(1734125284466830208)
XLA Ops:
  0.0 0.0 copy-start
  0.0 39.7 %shard_map.136 = f32[32,256]{1,0:T(8,128)} custom-call(s32[4,32]{1,0:T(4,128)} %bitcast.15, s32[32]{0:T(128)} %live_hbm.1, f32[32,4,256]{2,1,0:T(4,128)} %src_hbm.1, f32[32,296]{1,0:T(8,128)} %bitcast.10, s32[16,32]{1,0:T(8,128)} %bitcast.11, s32[16,32]{1,0:T(8,128)} %bitcast.12, s32[8,32]{1,0:T(8,128)} %bitcast.13, s32[8,32]{1,0:T(8,128)} %bitcast.14, ...), custom_call_target="tpu_custom_call" | custom-call | tf_op jit(solution)/shard_map/pallas_call | solution.py:453
  39.7 0.0 copy-done
  39.7 1.4 %fusion = f32[32,256]{1,0:T(8,128)} fusion(f32[32,256]{1,0:T(8,128)} %shard_map.136, s32[32]{0:T(128)S(1)} %copy-done), kind=kLoop, calls=%fused_computation.1 | loop fusion | flops 16384 | bytes 65664 | tf_op jit(solution)/shard_map/jit(_where)/select_n | solution.py:499
Async XLA Ops:
  0.0 39.7 %copy-start = (s32[32]{0:T(128)S(1)}, s32[32]{0:T(128)}, u32[]{:S(2)}) copy-start(s32[32]{0:T(128)} %live_hbm.1) | copy-start | bytes 388

commit v6 on v4

--- a/solution.py
+++ b/solution.py
@@ -486,7 +486,7 @@
             dma((3,)), dma((3,)), dma((4, 3)), dma((4, 3)), dma((16,)), dma((16,)), dma((14,)),
         ],
         compiler_params=pltpu.CompilerParams(
-            collective_id=0, has_side_effects=True, vmem_limit_bytes=60 * 1024 * 1024
+            collective_id=0, has_side_effects=True, vmem_limit_bytes=57 * 1024 * 1024
         ),
     )(
         near_list.T, live_counts, sources, densities.T, far_list.T, far_class.T, coarse_list.T, coarse_class.T,

time: 41 us -> 41 us (level)
  no operation moved by 1% of the time
where the time goes in v6:
time: 41 us; the launch traced here: 40.9 us
  Pallas kernels  39.4 us (96%)
  other arithmetic  1.45 us (4%)
    pallas_call x1, Pallas kernels, on_device(): pl.pallas_call(fmm_kernel, out_shape=jax.ShapeDtypeStruct((32, 256), f32)...  39.4 us
    select_n x1, other arithmetic, on_device(): jnp.where(jnp.arange(256, dtype=jnp.int32)[None, :] < live_counts[:, None...  1.45 us

profile of v6, /device:TPU:1, one launch (start us, length us, event | category | flops | bytes accessed | tf_op | source)
XLA Modules:
  0.0 40.9 jit_solution(645551868230273408)
XLA Ops:
  0.0 0.0 copy-start
  0.0 39.4 %shard_map.136 = f32[32,256]{1,0:T(8,128)} custom-call(s32[4,32]{1,0:T(4,128)} %bitcast.15, s32[32]{0:T(128)} %live_hbm.1, f32[32,4,256]{2,1,0:T(4,128)} %src_hbm.1, f32[32,296]{1,0:T(8,128)} %bitcast.10, s32[16,32]{1,0:T(8,128)} %bitcast.11, s32[16,32]{1,0:T(8,128)} %bitcast.12, s32[8,32]{1,0:T(8,128)} %bitcast.13, s32[8,32]{1,0:T(8,128)} %bitcast.14, ...), custom_call_target="tpu_custom_call" | custom-call | tf_op jit(solution)/shard_map/pallas_call | solution.py:449
  39.4 0.0 copy-done
  39.4 1.4 %fusion = f32[32,256]{1,0:T(8,128)} fusion(f32[32,256]{1,0:T(8,128)} %shard_map.136, s32[32]{0:T(128)S(1)} %copy-done), kind=kLoop, calls=%fused_computation.1 | loop fusion | flops 16384 | bytes 65664 | tf_op jit(solution)/shard_map/jit(_where)/select_n | solution.py:496
Async XLA Ops:
  0.0 39.4 %copy-start = (s32[32]{0:T(128)S(1)}, s32[32]{0:T(128)}, u32[]{:S(2)}) copy-start(s32[32]{0:T(128)} %live_hbm.1) | copy-start | bytes 388
